TPU v7x, 256 devices: a whole 4x4x8 slice. The times are simulated.
256 devices in a mesh: rep: 16 (over x, z_hi), tp: 16 (over z_lo, y, core).
Axes of the slice: x: 4, y: 4, z: 8 (z_hi: 4, z_lo: 2; z = z_hi * 2 + z_lo), core: 2. Of those that a mesh axis runs over, the one named last changes fastest.
Arguments:
- hidden: bfloat16 [32768, 8192], P('rep', 'tp'), may hold values from -0.0625 to 0.0625
- target: bfloat16 [32768, 1024], P('rep'), may hold values from -6 to 6
- inner_weight: bfloat16 [16, 8192, 1024], P('rep', 'tp'), as said below
- first_moment: float32 [16, 8192, 1024], P('rep', 'tp'), may hold values from -1.5 to 1.5
- second_moment: float32 [16, 8192, 1024], P('rep', 'tp'), may hold values from 0.001 to 0.01
- anchor: float32 [16, 512, 1024], P('tp', 'rep')
- outer_momentum: float32 [16, 512, 1024], P('tp', 'rep'), may hold values from -1.5 to 1.5
Outputs:
- fragment: bfloat16 [8192, 1024], P('tp')
- momentum_new: float32 [16, 512, 1024], P('tp', 'rep')
Inputs may be any that keep to these rules, and one draw needn't show every extreme that they name: `inner_weight`: each replica's inner weights are the anchor plus a drift of their own.
All inputs are finite; a program needn't handle non-finite values.
Results may differ from a plain program's by a relative error of at most 0.0017.
Values may be sent and summed in bfloat16 or wider, within the bound.
No kernel may reach another device: no remote copies, remote signals or barrier semaphores. Data moves between devices by JAX's collectives and lax.ppermute only.
A program may use at most 64 MiB of HBM per device.

v0:
```python
import jax
import jax.numpy as jnp
from jax import lax
from jax.sharding import PartitionSpec as P

beta_one = 0.9
beta_two = 0.999
inner_rate = 0.2
decay_rate = 0.1
outer_rate = 0.7
outer_mu = 0.9
adam_eps = 1e-08


def local(hidden, target, inner_weight, first_moment, second_moment, anchor, outer_momentum):
    weight = inner_weight[0]
    partial_value = jnp.dot(hidden, weight, preferred_element_type=jnp.float32)
    summed = lax.psum_scatter(
        partial_value.astype(jnp.bfloat16), "tp", scatter_dimension=0, tiled=True
    ).astype(jnp.float32)
    count = summed.shape[0]
    goal = lax.dynamic_slice_in_dim(target, lax.axis_index("tp") * count, count, 0)
    residual = (summed - goal.astype(jnp.float32)).astype(jnp.bfloat16)
    grad = lax.dot_general(
        hidden,
        lax.all_gather(residual, "tp", axis=0, tiled=True),
        (((0,), (0,)), ((), ())),
        preferred_element_type=jnp.float32,
    )
    moment_one = beta_one * first_moment[0] + (1.0 - beta_one) * grad
    moment_two = beta_two * second_moment[0] + (1.0 - beta_two) * grad * grad
    corr_one = 1.0 - beta_one**3
    corr_two = 1.0 - beta_two**3
    weight_f = weight.astype(jnp.float32)
    step_dir = moment_one / corr_one / (jnp.sqrt(moment_two / corr_two) + adam_eps)
    updated = weight_f - inner_rate * (step_dir + decay_rate * weight_f)
    replicas = lax.axis_size("rep")
    replica_mean = lax.psum_scatter(updated, "rep", scatter_dimension=0, tiled=True) / replicas
    anchor_rows = anchor[0]
    delta = anchor_rows - replica_mean
    momentum_new = outer_mu * outer_momentum[0] + delta
    piece = (anchor_rows - outer_rate * (delta + outer_mu * momentum_new)).astype(jnp.bfloat16)
    fragment = lax.all_gather(piece, "rep", axis=0, tiled=True)
    return (fragment, momentum_new[None])


def solution(mesh):
    placed = (
        P("rep", "tp"),
        P("rep", None),
        P("rep", "tp", None),
        P("rep", "tp", None),
        P("rep", "tp", None),
        P("tp", "rep", None),
        P("tp", "rep", None),
    )
    return jax.shard_map(
        local,
        mesh=mesh,
        in_specs=placed,
        out_specs=(P("tp", None), P("tp", "rep", None)),
        check_vma=False,
    )
```

profile of v0, /device:TPU:8, one launch (start us, length us, event | category | flops | bytes accessed | tf_op | source)
XLA Modules:
  0.0 292.7 jit_solution(12165705362500873506)
XLA Ops:
  7.2 0.0 copy-start
  7.2 0.0 reduce-scatter.5.cloned.1.call-start
  7.2 1.5 copy-done
  8.8 5.5 %convolution_convert_fusion = bf16[2048,1024]{1,0:T(8,128)(2,1)} fusion(bf16[2048,512]{1,0:T(8,128)(2,1)S(1)} %copy-done, bf16[1,512,1024]{2,1,0:T(8,128)(2,1)} %param.9), kind=kOutput, calls=%fused_computation | convolution fusion | flops 2149580800 | bytes 7340032 | tf_op jit(solution)/shard_map/dot_general | solution.py:17
  14.3 0.0 copy-start.1
  14.3 0.0 reduce-scatter.5.cloned.1.call-update
  14.3 0.0 all-gather.3.cloned.1.call-start
  14.4 68.8 %reduce-scatter.5.cloned.1.call-done = bf16[128,1024]{1,0:T(8,128)(2,1)} async-done(((bf16[2048,1024]{1,0:T(8,128)(2,1)}), bf16[128,1024]{1,0:T(8,128)(2,1)}) %reduce-scatter.5.cloned.1.call-update) | async-done | bytes 262160 | tf_op jit(solution)/shard_map/reduce_scatter | solution.py:18
  83.2 1.8 subtract_convert_fusion
  85.0 0.0 all-gather.3.cloned.1.call-update
  85.1 0.0 reduce-scatter.7.cloned.1.call-start
  85.1 0.0 copy-done.1
  85.1 1.3 copy.17
  86.4 2.9 copy.18
  89.3 0.0 copy-start.2
  89.3 3.0 %copy.19 = f32[1,512,1024]{1,2,0:T(8,128)} copy(f32[1,512,1024]{2,1,0:T(8,128)} %param.11) | data formatting | bytes 4194304 | tf_op args[4]
  92.4 34.4 %all-gather.3.cloned.1.call-done = bf16[2048,1024]{1,0:T(8,128)(2,1)} async-done(((bf16[128,1024]{1,0:T(8,128)(2,1)}), bf16[2048,1024]{1,0:T(8,128)(2,1)}) %all-gather.3.cloned.1.call-update) | async-done | bytes 4194320 | tf_op jit(solution)/shard_map/all_gather | solution.py:26
  126.8 0.0 copy-done.2
  126.8 8.6 %convert_subtract_fusion = f32[512,1024]{0,1:T(8,128)} fusion(f32[1,512,1024]{1,2,0:T(8,128)} %copy.19, f32[1,512,1024]{1,2,0:T(8,128)} %copy.18, bf16[2048,1024]{1,0:T(8,128)(2,1)} %all-gather.3.cloned.1.call-done, bf16[2048,512]{1,0:T(8,128)(2,1)S(1)} %copy-done, bf16[1,512,1024]{1,2,0:T(8,128)(2,1)S(1)} %copy-done.2), kind=kOutput, calls=%fused_computation.2 | convolution fusion | flops 2155872256 | bytes 13631488 | tf_op jit(solution)/shard_map/dot_general | solution.py:24
  135.3 2.9 copy.23
  138.3 0.0 copy-start.3
  138.3 0.0 copy-start.4
  138.3 0.0 reduce-scatter.7.cloned.1.call-update
  138.3 0.0 all-gather.5.cloned.1.call-start
  138.3 0.8 copy-done.3
  139.2 0.2 copy.16
  139.4 0.0 copy-done.4
  139.4 1.0 copy.20
  140.4 88.4 %reduce-scatter.7.cloned.1.call-done = f32[32,1024]{1,0:T(8,128)} async-done(((f32[512,1024]{1,0:T(8,128)}), f32[32,1024]{1,0:T(8,128)}) %reduce-scatter.7.cloned.1.call-update) | async-done | bytes 131088
  228.8 1.9 copy.24
  230.7 1.4 fusion.11
  232.1 0.8 copy.21
  232.8 0.0 all-gather.5.cloned.1.call-update
  232.9 0.8 copy.22
  233.7 50.2 %all-gather.5.cloned.1.call-done = bf16[512,1024]{1,0:T(8,128)(2,1)} async-done(((bf16[32,1024]{1,0:T(8,128)(2,1)}), bf16[512,1024]{1,0:T(8,128)(2,1)}) %all-gather.5.cloned.1.call-update) | async-done | bytes 1048592 | tf_op jit(solution)/shard_map/all_gather | solution.py:43
  283.9 2.3 copy.26
Async XLA Ops:
  7.2 1.6 copy-start
  7.2 76.0 %reduce-scatter.5.cloned.1.call-start = ((), (), s32[]{:S(2)}) async-start(), calls=%async_computation.2 | async-start | bytes 4456448 | tf_op jit(solution)/shard_map/reduce_scatter | solution.py:18
  14.3 70.8 %copy-start.1 = (bf16[1,512,1024]{2,1,0:T(8,128)(2,1)S(1)}, bf16[1,512,1024]{2,1,0:T(8,128)(2,1)}, u32[]{:S(2)}) copy-start(bf16[1,512,1024]{2,1,0:T(8,128)(2,1)} %param.9) | copy-start | bytes 3145732
  14.3 112.5 %all-gather.3.cloned.1.call-start = ((), (), s32[]{:S(2)}) async-start(), calls=%async_computation.3 | async-start | bytes 4456448 | tf_op jit(solution)/shard_map/all_gather | solution.py:26
  85.1 143.8 %reduce-scatter.7.cloned.1.call-start = ((), (), s32[]{:S(2)}) async-start(), calls=%async_computation.5 | async-start | bytes 2228224
  89.3 37.4 %copy-start.2 = (bf16[1,512,1024]{1,2,0:T(8,128)(2,1)S(1)}, bf16[1,512,1024]{1,2,0:T(8,128)(2,1)}, u32[]{:S(2)}) copy-start(bf16[1,512,1024]{1,2,0:T(8,128)(2,1)} %copy.17) | copy-start | bytes 3145732
  138.3 0.9 copy-start.3
  138.3 1.1 copy-start.4
  138.3 145.6 %all-gather.5.cloned.1.call-start = ((), (), s32[]{:S(2)}) async-start(), calls=%async_computation.4 | async-start | bytes 1114112 | tf_op jit(solution)/shard_map/all_gather | solution.py:43
Sparse Core Ops, SparseCore 0:
  14.4 68.7 reduce-scatter.4
  85.2 41.5 all-gather.2
  138.4 90.3 reduce-scatter.6
  233.0 50.9 all-gather.4
where the time goes:
time: 293 us
  waiting for transfers between devices  242 us (83%)
  local copies, waits for them, and re-layouts  19.5 us (7%)
  matrix products  14.1 us (5%)
  between operations  13.8 us (5%)
  other arithmetic  3.19 us (1%)
    unnamed x5, waiting for transfers between devices  88.5 us
    reduce_scatter x1, waiting for transfers between devices, local(): lax.psum_scatter(partial_value.astype(jnp.bfloat16), 'tp', scatter_dimens...  68.8 us
    all_gather x1, waiting for transfers between devices, local(): fragment = lax.all_gather(piece, 'rep', axis=0, tiled=True)  50.2 us
    all_gather x1, waiting for transfers between devices, local(): lax.all_gather(residual, 'tp', axis=0, tiled=True)  34.4 us
    unnamed x19, local copies, waits for them, and re-layouts  18.7 us
    dot_general x1, matrix products, local(): lax.dot_general(hidden, lax.all_gather(residual, 'tp', axis=0, tiled=True...  8.58 us
  transfers between devices with their start and end apart: 4, of which 4 were waited for; matrix products, arithmetic and copies ran while one was open for 3% of the time, Pallas kernels for 0%

commit v1 on v0

v1 whole, which is shorter than its diff:
```python
import jax
import jax.numpy as jnp
from jax import lax
from jax.experimental import pallas as pl
from jax.experimental.pallas import tpu as pltpu
from jax.sharding import PartitionSpec as P

beta_one = 0.9
beta_two = 0.999
inner_rate = 0.2
decay_rate = 0.1
outer_rate = 0.7
outer_mu = 0.9
adam_eps = 1e-08

f32 = jnp.float32
bf16 = jnp.bfloat16


CHIPS = [[chip * 2 + core for chip in range(8)] for core in range(2)]


def spread(x, axis, groups=None):
    return lax.all_to_all(x, axis, 0, 0, axis_index_groups=groups)


def swap(x, axis, mask):
    return lax.ppermute(x, axis, [(i, i ^ mask) for i in range(16)])


def turn(x, by):
    return lax.ppermute(x, "rep", [(i, i // 4 * 4 + (i + by) % 4) for i in range(16)])


def part(x, at, parts):
    size = x.shape[0] // parts
    return lax.dynamic_slice_in_dim(x, at * size, size, 0)


def residual_kernel(at_ref, parts_ref, goal_ref, wide_ref):
    total = parts_ref[0].astype(f32)
    for i in range(1, parts_ref.shape[0]):
        total = total + parts_ref[i].astype(f32)
    residual = (total - goal_ref[...].astype(f32)).astype(bf16)
    for i in range(wide_ref.shape[0]):
        wide_ref[i] = residual


def residual_copies(parts, target, at, steps=4):
    copies, rows, cols = parts.shape
    size = rows // steps
    return pl.pallas_call(
        residual_kernel,
        out_shape=jax.ShapeDtypeStruct(parts.shape, bf16),
        grid_spec=pltpu.PrefetchScalarGridSpec(
            num_scalar_prefetch=1,
            grid=(steps,),
            in_specs=[
                pl.BlockSpec((copies, size, cols), lambda i, at: (0, i, 0)),
                pl.BlockSpec((size, cols), lambda i, at: (at[0] * steps + i, 0)),
            ],
            out_specs=pl.BlockSpec((copies, size, cols), lambda i, at: (0, i, 0)),
        ),
        cost_estimate=pl.CostEstimate(flops=copies * rows * cols, bytes_accessed=4 * copies * rows * cols, transcendentals=0),
        name="residual",
    )(at.reshape(1).astype(jnp.int32), parts, target)


def scaled_part(x, at, parts, by):
    rows, cols = x.shape[0] // parts, x.shape[1]

    def kernel(at_ref, x_ref, out_ref):
        out_ref[...] = x_ref[...] * by

    return pl.pallas_call(
        kernel,
        out_shape=jax.ShapeDtypeStruct((rows, cols), x.dtype),
        grid_spec=pltpu.PrefetchScalarGridSpec(
            num_scalar_prefetch=1,
            grid=(1,),
            in_specs=[pl.BlockSpec((rows, cols), lambda i, at: (at[0], 0))],
            out_specs=pl.BlockSpec((rows, cols), lambda i, at: (0, 0)),
        ),
        cost_estimate=pl.CostEstimate(flops=rows * cols, bytes_accessed=8 * rows * cols, transcendentals=0),
        name="scaled_part",
    )(at.reshape(1).astype(jnp.int32), x)


def local(hidden, target, inner_weight, first_moment, second_moment, anchor, outer_momentum):
    weight = inner_weight[0]
    cols = weight.shape[1]
    tp, rep = lax.axis_index("tp"), lax.axis_index("rep")
    core, chip = tp % 2, tp // 2
    half = hidden.shape[0] // 2
    mine, other = part(hidden, core, 2), part(hidden, 1 - core, 2)

    give = part(weight, 1 - rep // 8, 2)
    got = swap(give, "rep", 12)
    w_x = part(weight, rep // 8, 2).astype(f32) + got.astype(f32)
    give = part(w_x, 1 - rep // 4 % 2, 2)
    got = swap(give, "rep", 4)
    w_x = part(w_x, rep // 4 % 2, 2) + got
    w_sum = scaled_part(w_x, rep % 4, 4, 1.0 - inner_rate * decay_rate)
    for by in (2, 1, 3):
        give = part(w_x, (rep + by) % 4, 4)
        got = turn(give, by)
        w_sum = w_sum + got * (1.0 - inner_rate * decay_rate)

    w_other = swap(weight, "tp", 1)
    h_other = swap(other, "tp", 1)
    own = jnp.dot(mine, weight, preferred_element_type=f32)
    pair_sum = (own + jnp.dot(h_other, w_other, preferred_element_type=f32)).astype(bf16)
    parts = spread(pair_sum.reshape(8, half // 8, cols), "tp", CHIPS)
    wide = residual_copies(parts, target, core * 8 + chip)
    res = spread(wide, "tp", CHIPS).reshape(half, cols)
    dims = (((0,), (0,)), ((), ()))
    corr_one = 1.0 - beta_one**3
    corr_two = 1.0 - beta_two**3
    res_other = swap(res, "tp", 1)
    grad = lax.dot_general(mine, res, dims, preferred_element_type=f32)
    grad = grad + lax.dot_general(other, res_other, dims, preferred_element_type=f32)
    moment_one = beta_one * first_moment[0] + (1.0 - beta_one) * grad
    moment_two = beta_two * second_moment[0] + (1.0 - beta_two) * grad * grad
    step_dir = (moment_one / corr_one / (jnp.sqrt(moment_two / corr_two) + adam_eps)).astype(bf16)
    steps = spread(step_dir.reshape(16, 32, cols), "rep")
    updated = w_sum - inner_rate * jnp.sum(steps.astype(f32), axis=0)
    anchor_rows = anchor[0]
    delta = anchor_rows - updated / 16.0
    momentum_new = outer_mu * outer_momentum[0] + delta
    piece = (anchor_rows - outer_rate * (delta + outer_mu * momentum_new)).astype(bf16)
    wide = jnp.broadcast_to(piece[None], (16,) + piece.shape)
    fragment = spread(wide, "rep").reshape(512, cols)
    return (fragment, momentum_new[None])


def solution(mesh):
    placed = (
        P("rep", "tp"),
        P("rep", None),
        P("rep", "tp", None),
        P("rep", "tp", None),
        P("rep", "tp", None),
        P("tp", "rep", None),
        P("tp", "rep", None),
    )

    return jax.shard_map(
        local,
        mesh=mesh,
        in_specs=placed,
        out_specs=(P("tp", None), P("tp", "rep", None)),
        check_vma=False,
    )
```

time: 293 us -> 197 us (0.67)
  waiting for transfers between devices: 242 us -> 71.1 us
  blocking collectives: 0 us -> 62.3 us
  starting transfers between devices: 0.16 us -> 30.7 us
  between operations: 13.8 us -> 0.78 us
  local copies, waits for them, and re-layouts: 19.5 us -> 8.02 us
  Pallas kernels: 0 us -> 5.49 us
    unnamed x5 -> x0, waiting for transfers between devices: 88.5 us -> none
    all_gather x2 -> x0, waiting for transfers between devices: 84.7 us -> none  [the longest x1 50.2 us: local(): fragment = lax.all_gather(piece, 'rep', axis=0, tiled=True)]
    reduce_scatter x1 -> x0, waiting for transfers between devices: 68.8 us -> none  [local(): lax.psum_scatter(partial_value.astype(jnp.bfloat16), 'tp', scatter_dimens...]
    all_to_all x0 -> x2, blocking collectives: none -> 62.3 us  [spread(): return lax.all_to_all(x, axis, 0, 0, axis_index_groups=groups)]
    ppermute x0 -> x8, waiting for transfers between devices: none -> 45.6 us  [the longest x5 37 us: swap(): return lax.ppermute(x, axis, [(i, i ^ mask) for i in range(16)])]
    all_to_all x0 -> x2, waiting for transfers between devices: none -> 25.6 us  [spread(): return lax.all_to_all(x, axis, 0, 0, axis_index_groups=groups)]
    all_to_all x0 -> x2, starting transfers between devices: none -> 16.1 us  [spread(): return lax.all_to_all(x, axis, 0, 0, axis_index_groups=groups)]
    ppermute x0 -> x8, starting transfers between devices: none -> 14.6 us  [the longest x3 9.77 us: turn(): lax.ppermute(x, 'rep', [(i, i // 4 * 4 + (i + by) % 4) for i in range(16)])]
  transfers between devices with their start and end apart: 4 -> 10, of which waited for: 4 -> 7; matrix products, arithmetic and copies ran while one was open for 3% -> 5% of each run, Pallas kernels for 0% -> 1%
where the time goes in v1:
time: 197 us; the launch traced here: 194 us
  waiting for transfers between devices  71.1 us (36%)
  blocking collectives  62.3 us (32%)
  starting transfers between devices  30.7 us (16%)
  matrix products  11.4 us (6%)
  local copies, waits for them, and re-layouts  8.02 us (4%)
  Pallas kernels  5.49 us (3%)
  other arithmetic  4.6 us (2%)
    all_to_all x2, blocking collectives, spread(): return lax.all_to_all(x, axis, 0, 0, axis_index_groups=groups)  62.3 us
    ppermute x5, waiting for transfers between devices, swap(): return lax.ppermute(x, axis, [(i, i ^ mask) for i in range(16)])  37 us
    all_to_all x2, waiting for transfers between devices, spread(): return lax.all_to_all(x, axis, 0, 0, axis_index_groups=groups)  25.6 us
    all_to_all x2, starting transfers between devices, spread(): return lax.all_to_all(x, axis, 0, 0, axis_index_groups=groups)  16.1 us
    ppermute x3, starting transfers between devices, turn(): lax.ppermute(x, 'rep', [(i, i // 4 * 4 + (i + by) % 4) for i in range(16)])  9.77 us
    ppermute x3, waiting for transfers between devices, turn(): lax.ppermute(x, 'rep', [(i, i // 4 * 4 + (i + by) % 4) for i in range(16)])  8.54 us
    ppermute x5, starting transfers between devices, swap(): return lax.ppermute(x, axis, [(i, i ^ mask) for i in range(16)])  4.83 us
    unnamed x15, local copies, waits for them, and re-layouts  4.33 us
  transfers between devices with their start and end apart: 10, of which 7 were waited for; matrix products, arithmetic and copies ran while one was open for 5% of the time, Pallas kernels for 1%

profile of v1, /device:TPU:8, one launch (start us, length us, event | category | flops | bytes accessed | tf_op | source)
XLA Modules:
  0.0 194.4 jit_solution(3022506540697981312)
XLA Ops:
  0.6 0.0 copy-start
  0.7 1.6 copy-done
  2.2 0.1 constant_dynamic-slice_fusion
  2.3 0.1 collective-permute-start.5
  2.4 0.5 collective-permute-start.6
  2.9 2.5 %fusion.9 = f32[1024,1024]{1,0:T(8,128)S(1)} fusion(bf16[2048,512]{1,0:T(8,128)(2,1)S(1)} %copy-done, s32[]{:T(128)S(6)} %select_n.83, bf16[1,512,1024]{2,1,0:T(8,128)(2,1)} %param.9), kind=kOutput, calls=%fused_computation.14 | convolution fusion | flops 1073741824 | bytes 6291460 | tf_op jit(solution)/shard_map/dot_general | solution.py:111
  5.4 0.0 collective-permute-done.5
  5.4 1.3 collective-permute-done.6
  6.7 4.2 %add_convert_fusion = bf16[1024,1024]{1,0:T(8,128)(2,1)} fusion(f32[1024,1024]{1,0:T(8,128)S(1)} %fusion.9, bf16[1024,512]{1,0:T(8,128)(2,1)} %collective-permute-done.5, bf16[512,1024]{1,0:T(8,128)(2,1)} %collective-permute-done.6), kind=kOutput, calls=%fused_computation | convolution fusion | flops 1075838976 | bytes 8388608 | tf_op jit(solution)/shard_map/dot_general | solution.py:112
  10.8 6.4 %all-to-all-start = ((bf16[8,128,1024]{2,1,0:T(8,128)(2,1)}), bf16[8,128,1024]{2,1,0:T(8,128)(2,1)}, u32[]{:S(2)}, u32[]{:S(2)}) async-start(bf16[8,128,1024]{2,1,0:T(8,128)(2,1)} %bitcast.47), calls=%async_computation | async-start | bytes 4194304 | tf_op jit(solution)/shard_map/all_to_all | solution.py:24
  17.2 25.6 %all-to-all-done.parts_ref = bf16[8,128,1024]{2,1,0:T(8,128)(2,1)} async-done(((bf16[8,128,1024]{2,1,0:T(8,128)(2,1)}), bf16[8,128,1024]{2,1,0:T(8,128)(2,1)}, u32[]{:S(2)}, u32[]{:S(2)}) %all-to-all-start) | async-done | bytes 2097184 | tf_op jit(solution)/shard_map/all_to_all | solution.py:24
  42.8 3.9 %residual.1 = bf16[8,128,1024]{2,1,0:T(8,128)(2,1)} custom-call(s32[1]{0:T(128)} %bitcast.5.at_ref, bf16[8,128,1024]{2,1,0:T(8,128)(2,1)} %all-to-all-done.parts_ref, bf16[2048,1024]{1,0:T(8,128)(2,1)} %goal_ref.1), custom_call_target="tpu_custom_call" | custom-call | flops 1048576 | bytes 4194304 | tf_op jit(solution)/shard_map/residual/pallas_call | solution.py:52
  46.7 30.3 %all_to_all.20 = bf16[8,128,1024]{2,1,0:T(8,128)(2,1)S(1)} all-to-all(bf16[8,128,1024]{2,1,0:T(8,128)(2,1)} %residual.1), channel_id=1, replica_groups={{0,2,4,6,8,10,12,14},{1,3,5,7,9,11,13,15},{16,18,20,22,24,26,28,30},{17..., dimensions={0} | all-to-all | bytes 4194304 | tf_op jit(solution)/shard_map/all_to_all | solution.py:24
  77.0 0.0 collective-permute-start.7
  77.0 1.3 fusion.7
  78.3 2.9 %collective-permute-done.7 = bf16[1024,1024]{1,0:T(8,128)(2,1)S(1)} collective-permute-done((bf16[1024,1024]{1,0:T(8,128)(2,1)S(1)}, bf16[1024,1024]{1,0:T(8,128)(2,1)S(1)}, u32[]{:S(2)}, u32[]{:S(2)}) %collective-permute-start.7) | collective-permute-done | bytes 2097184 | tf_op jit(solution)/shard_map/ppermute | solution.py:28
  81.2 0.0 copy-done.5
  81.2 0.0 copy-done.6
  81.2 3.5 %fusion.6 = bf16[512,1024]{1,0:T(8,128)(2,1)} fusion(f32[1,512,1024]{2,1,0:T(8,128)S(1)} %copy-done.5, f32[512,1024]{1,0:T(8,128)S(1)} %fusion.7, f32[1,512,1024]{2,1,0:T(8,128)S(1)} %copy-done.6, bf16[1024,512]{1,0:T(8,128)(2,1)S(1)} %constant_dynamic-slice_fusion, bf16[1024,1024]{1,0:T(8,128)(2,1)S(1)} %collective-permute-done.7), kind=kOutput, calls=%fused_computation.10 | convolution fusion | flops 1080557568 | bytes 10485760 | tf_op jit(solution)/shard_map/dot_general | solution.py:121
  84.7 9.7 %all-to-all-start.2 = ((bf16[16,32,1024]{2,1,0:T(8,128)(2,1)}), bf16[16,32,1024]{2,1,0:T(8,128)(2,1)S(1)}, u32[]{:S(2)}, u32[]{:S(2)}) async-start(bf16[16,32,1024]{2,1,0:T(8,128)(2,1)} %bitcast.49), calls=%async_computation.2 | async-start | bytes 2097152 | tf_op jit(solution)/shard_map/all_to_all | solution.py:24
  94.4 1.9 dynamic-slice_bitcast_fusion
  96.3 3.1 %collective-permute-start = (bf16[256,1024]{1,0:T(8,128)(2,1)}, bf16[256,1024]{1,0:T(8,128)(2,1)}, u32[]{:S(2)}, u32[]{:S(2)}) collective-permute-start(bf16[256,1024]{1,0:T(8,128)(2,1)} %dynamic-slice_bitcast_fusion), channel_id=1, source_target_pairs={{0,192},{16,208},{32,224},{48,240},{64,128},{80,144},{96,160},{112... | collective-permute-start | bytes 1572872 | tf_op jit(solution)/shard_map/ppermute | solution.py:28
  99.4 20.4 %collective-permute-done = bf16[256,1024]{1,0:T(8,128)(2,1)} collective-permute-done((bf16[256,1024]{1,0:T(8,128)(2,1)}, bf16[256,1024]{1,0:T(8,128)(2,1)}, u32[]{:S(2)}, u32[]{:S(2)}) %collective-permute-start) | collective-permute-done | bytes 524320 | tf_op jit(solution)/shard_map/ppermute | solution.py:28
  119.9 1.4 convert_add_fusion
  121.3 0.0 copy-start.1
  121.3 1.0 copy-done.1
  122.2 0.9 constant_dynamic-slice_fusion.4
  123.1 1.1 collective-permute-start.1
  124.2 12.4 %collective-permute-done.1 = f32[128,1024]{1,0:T(8,128)} collective-permute-done((f32[128,1024]{1,0:T(8,128)}, f32[128,1024]{1,0:T(8,128)}, u32[]{:S(2)}, u32[]{:S(2)}) %collective-permute-start.1) | collective-permute-done | bytes 524320 | tf_op jit(solution)/shard_map/ppermute | solution.py:28
  136.7 1.3 dynamic-slice_add_fusion.x_ref
  137.9 0.0 copy-start.2
  137.9 0.8 copy-done.2
  138.7 0.8 constant_dynamic-slice_fusion.3
  139.5 5.1 %collective-permute-start.4 = (f32[32,1024]{1,0:T(8,128)}, f32[32,1024]{1,0:T(8,128)S(1)}, u32[]{:S(2)}, u32[]{:S(2)}) collective-permute-start(f32[32,1024]{1,0:T(8,128)} %get-tuple-element.5), channel_id=1, source_target_pairs={{0,48},{16,0},{32,16},{48,32},{64,112},{80,64},{96,80},{112,96},{1... | collective-permute-start | bytes 393224 | tf_op jit(solution)/shard_map/ppermute | solution.py:32
  144.6 0.0 collective-permute-start.3
  144.6 1.6 scaled_part.1
  146.2 4.6 %collective-permute-start.2 = (f32[32,1024]{1,0:T(8,128)}, f32[32,1024]{1,0:T(8,128)}, u32[]{:S(2)}, u32[]{:S(2)}) collective-permute-start(f32[32,1024]{1,0:T(8,128)} %get-tuple-element.4), channel_id=1, source_target_pairs={{0,32},{16,48},{32,0},{48,16},{64,96},{80,112},{96,64},{112,80},{1... | collective-permute-start | bytes 393224 | tf_op jit(solution)/shard_map/ppermute | solution.py:32
  150.8 0.0 all-to-all-done.2
  150.8 0.2 convert_reduce_fusion
  151.0 0.0 collective-permute-done.4
  151.0 3.5 %collective-permute-done.3 = f32[32,1024]{1,0:T(8,128)} collective-permute-done((f32[32,1024]{1,0:T(8,128)}, f32[32,1024]{1,0:T(8,128)}, u32[]{:S(2)}, u32[]{:S(2)}) %collective-permute-start.3) | collective-permute-done | bytes 131104 | tf_op jit(solution)/shard_map/ppermute | solution.py:32
  154.6 5.0 %collective-permute-done.2 = f32[32,1024]{1,0:T(8,128)} collective-permute-done((f32[32,1024]{1,0:T(8,128)}, f32[32,1024]{1,0:T(8,128)}, u32[]{:S(2)}, u32[]{:S(2)}) %collective-permute-start.2) | collective-permute-done | bytes 131104 | tf_op jit(solution)/shard_map/ppermute | solution.py:32
  159.6 0.0 copy-done.3
  159.6 0.0 copy-done.4
  159.6 1.8 fusion.12
  161.4 0.1 broadcast_in_dim.4
  161.5 32.0 %all_to_all.21 = bf16[16,32,1024]{2,1,0:T(8,128)(2,1)S(1)} all-to-all(bf16[16,32,1024]{2,1,0:T(8,128)(2,1)S(1)} %broadcast_in_dim.4), channel_id=1, replica_groups=mesh['rep'=16,'tp'=16] {'rep'}, dimensions={0} | all-to-all | bytes 2097152 | tf_op jit(solution)/shard_map/all_to_all | solution.py:24
  193.5 1.0 copy.10
  (5 shorter events, 0.0 us)
Async XLA Ops:
  0.6 1.6 copy-start
  2.3 3.1 %collective-permute-start.5 = (bf16[1024,512]{1,0:T(8,128)(2,1)S(1)}, bf16[1024,512]{1,0:T(8,128)(2,1)}, u32[]{:S(2)}, u32[]{:S(2)}) collective-permute-start(bf16[1024,512]{1,0:T(8,128)(2,1)S(1)} %constant_dynamic-slice_fusion), channel_id=1, source_target_pairs={{0,1},{1,0},{2,3},{3,2},{4,5},{5,4},{6,7},{7,6},{8,9},{9,8},{10,11... | collective-permute-start | bytes 3145736 | tf_op jit(solution)/shard_map/ppermute | solution.py:28
  2.4 4.3 %collective-permute-start.6 = (bf16[512,1024]{1,0:T(8,128)(2,1)}, bf16[512,1024]{1,0:T(8,128)(2,1)}, u32[]{:S(2)}, u32[]{:S(2)}) collective-permute-start(bf16[512,1024]{1,0:T(8,128)(2,1)} %bitcast.6), channel_id=1, source_target_pairs={{0,1},{1,0},{2,3},{3,2},{4,5},{5,4},{6,7},{7,6},{8,9},{9,8},{10,11... | collective-permute-start | bytes 3145736 | tf_op jit(solution)/shard_map/ppermute | solution.py:28
  10.8 32.0 %all-to-all-start = ((bf16[8,128,1024]{2,1,0:T(8,128)(2,1)}), bf16[8,128,1024]{2,1,0:T(8,128)(2,1)}, u32[]{:S(2)}, u32[]{:S(2)}) async-start(bf16[8,128,1024]{2,1,0:T(8,128)(2,1)} %bitcast.47), calls=%async_computation | async-start | bytes 4194304 | tf_op jit(solution)/shard_map/all_to_all | solution.py:24
  77.0 4.2 %copy-start.5 = (f32[1,512,1024]{2,1,0:T(8,128)S(1)}, f32[1,512,1024]{2,1,0:T(8,128)}, u32[]{:S(2)}) copy-start(f32[1,512,1024]{2,1,0:T(8,128)} %param.11) | copy-start | bytes 6291460
  77.0 4.2 %copy-start.6 = (f32[1,512,1024]{2,1,0:T(8,128)S(1)}, f32[1,512,1024]{2,1,0:T(8,128)}, u32[]{:S(2)}) copy-start(f32[1,512,1024]{2,1,0:T(8,128)} %param.10) | copy-start | bytes 6291460
  77.0 4.2 %collective-permute-start.7 = (bf16[1024,1024]{1,0:T(8,128)(2,1)S(1)}, bf16[1024,1024]{1,0:T(8,128)(2,1)S(1)}, u32[]{:S(2)}, u32[]{:S(2)}) collective-permute-start(bf16[1024,1024]{1,0:T(8,128)(2,1)S(1)} %bitcast.45), channel_id=1, source_target_pairs={{0,1},{1,0},{2,3},{3,2},{4,5},{5,4},{6,7},{7,6},{8,9},{9,8},{10,11... | collective-permute-start | bytes 6291464 | tf_op jit(solution)/shard_map/ppermute | solution.py:28
  84.7 66.1 %all-to-all-start.2 = ((bf16[16,32,1024]{2,1,0:T(8,128)(2,1)}), bf16[16,32,1024]{2,1,0:T(8,128)(2,1)S(1)}, u32[]{:S(2)}, u32[]{:S(2)}) async-start(bf16[16,32,1024]{2,1,0:T(8,128)(2,1)} %bitcast.49), calls=%async_computation.2 | async-start | bytes 2097152 | tf_op jit(solution)/shard_map/all_to_all | solution.py:24
  96.3 23.6 %collective-permute-start = (bf16[256,1024]{1,0:T(8,128)(2,1)}, bf16[256,1024]{1,0:T(8,128)(2,1)}, u32[]{:S(2)}, u32[]{:S(2)}) collective-permute-start(bf16[256,1024]{1,0:T(8,128)(2,1)} %dynamic-slice_bitcast_fusion), channel_id=1, source_target_pairs={{0,192},{16,208},{32,224},{48,240},{64,128},{80,144},{96,160},{112... | collective-permute-start | bytes 1572872 | tf_op jit(solution)/shard_map/ppermute | solution.py:28
  121.3 1.0 copy-start.1
  123.1 13.6 %collective-permute-start.1 = (f32[128,1024]{1,0:T(8,128)}, f32[128,1024]{1,0:T(8,128)}, u32[]{:S(2)}, u32[]{:S(2)}) collective-permute-start(f32[128,1024]{1,0:T(8,128)} %constant_dynamic-slice_fusion.4), channel_id=1, source_target_pairs={{0,64},{16,80},{32,96},{48,112},{64,0},{80,16},{96,32},{112,48},{1... | collective-permute-start | bytes 1572872 | tf_op jit(solution)/shard_map/ppermute | solution.py:28
  124.2 35.3 %copy-start.3 = (f32[1,32,1024]{2,1,0:T(8,128)S(1)}, f32[1,32,1024]{2,1,0:T(8,128)}, u32[]{:S(2)}) copy-start(f32[1,32,1024]{2,1,0:T(8,128)} %param.12) | copy-start | bytes 393220
  124.2 35.3 %copy-start.4 = (f32[1,32,1024]{2,1,0:T(8,128)S(1)}, f32[1,32,1024]{2,1,0:T(8,128)}, u32[]{:S(2)}) copy-start(f32[1,32,1024]{2,1,0:T(8,128)} %param.13) | copy-start | bytes 393220
  137.9 0.8 copy-start.2
  139.5 11.5 %collective-permute-start.4 = (f32[32,1024]{1,0:T(8,128)}, f32[32,1024]{1,0:T(8,128)S(1)}, u32[]{:S(2)}, u32[]{:S(2)}) collective-permute-start(f32[32,1024]{1,0:T(8,128)} %get-tuple-element.5), channel_id=1, source_target_pairs={{0,48},{16,0},{32,16},{48,32},{64,112},{80,64},{96,80},{112,96},{1... | collective-permute-start | bytes 393224 | tf_op jit(solution)/shard_map/ppermute | solution.py:32
  144.6 9.9 %collective-permute-start.3 = (f32[32,1024]{1,0:T(8,128)}, f32[32,1024]{1,0:T(8,128)}, u32[]{:S(2)}, u32[]{:S(2)}) collective-permute-start(f32[32,1024]{1,0:T(8,128)} %get-tuple-element.6), channel_id=1, source_target_pairs={{0,16},{16,32},{32,48},{48,0},{64,80},{80,96},{96,112},{112,64},{1... | collective-permute-start | bytes 393224 | tf_op jit(solution)/shard_map/ppermute | solution.py:32
  146.2 13.4 %collective-permute-start.2 = (f32[32,1024]{1,0:T(8,128)}, f32[32,1024]{1,0:T(8,128)}, u32[]{:S(2)}, u32[]{:S(2)}) collective-permute-start(f32[32,1024]{1,0:T(8,128)} %get-tuple-element.4), channel_id=1, source_target_pairs={{0,32},{16,48},{32,0},{48,16},{64,96},{80,112},{96,64},{112,80},{1... | collective-permute-start | bytes 393224 | tf_op jit(solution)/shard_map/ppermute | solution.py:32

commit v2 on v1

--- a/solution.py
+++ b/solution.py
@@ -17,6 +17,8 @@
 bf16 = jnp.bfloat16
 
 
+ROWS = [[x * 4 + z for x in range(4)] for z in range(4)]
+COLUMNS = [[x * 4 + z for z in range(4)] for x in range(4)]
 CHIPS = [[chip * 2 + core for chip in range(8)] for core in range(2)]
 
 
@@ -46,7 +48,7 @@
         wide_ref[i] = residual
 
 
-def residual_copies(parts, target, at, steps=4):
+def residual_copies(parts, target, at, steps=2):
     copies, rows, cols = parts.shape
     size = rows // steps
     return pl.pallas_call(
@@ -66,24 +68,35 @@
     )(at.reshape(1).astype(jnp.int32), parts, target)
 
 
-def scaled_part(x, at, parts, by):
-    rows, cols = x.shape[0] // parts, x.shape[1]
+def summed_parts(x, got, side, at, by):
+    rows, cols = got.shape
+    size = rows // 4
 
-    def kernel(at_ref, x_ref, out_ref):
-        out_ref[...] = x_ref[...] * by
+    def kernel(at_ref, x_ref, got_ref, own_ref, *part_refs):
+        def total(turned):
+            start = pl.multiple_of((at_ref[1] + turned) % 4 * size, size)
+            return x_ref[pl.ds(start, size), :] + got_ref[pl.ds(start, size), :]
 
+        own_ref[...] = total(0) * by
+        for turned, part_ref in enumerate(part_refs):
+            part_ref[...] = total(turned + 1)
+
+    piece = jax.ShapeDtypeStruct((size, cols), f32)
     return pl.pallas_call(
         kernel,
-        out_shape=jax.ShapeDtypeStruct((rows, cols), x.dtype),
+        out_shape=(piece,) * 4,
         grid_spec=pltpu.PrefetchScalarGridSpec(
             num_scalar_prefetch=1,
             grid=(1,),
-            in_specs=[pl.BlockSpec((rows, cols), lambda i, at: (at[0], 0))],
-            out_specs=pl.BlockSpec((rows, cols), lambda i, at: (0, 0)),
+            in_specs=[
+                pl.BlockSpec((rows, cols), lambda i, at: (at[0], 0)),
+                pl.BlockSpec((rows, cols), lambda i, at: (0, 0)),
+            ],
+            out_specs=(pl.BlockSpec((size, cols), lambda i, at: (0, 0)),) * 4,
         ),
-        cost_estimate=pl.CostEstimate(flops=rows * cols, bytes_accessed=8 * rows * cols, transcendentals=0),
-        name="scaled_part",
-    )(at.reshape(1).astype(jnp.int32), x)
+        cost_estimate=pl.CostEstimate(flops=rows * cols, bytes_accessed=12 * rows * cols, transcendentals=0),
+        name="summed_parts",
+    )(jnp.stack([side, at]).astype(jnp.int32), x, got)
 
 
 def local(hidden, target, inner_weight, first_moment, second_moment, anchor, outer_momentum):
@@ -99,17 +112,14 @@
     w_x = part(weight, rep // 8, 2).astype(f32) + got.astype(f32)
     give = part(w_x, 1 - rep // 4 % 2, 2)
     got = swap(give, "rep", 4)
-    w_x = part(w_x, rep // 4 % 2, 2) + got
-    w_sum = scaled_part(w_x, rep % 4, 4, 1.0 - inner_rate * decay_rate)
+    w_sum, *gives = summed_parts(w_x, got, rep // 4 % 2, rep % 4, 1.0 - inner_rate * decay_rate)
     for by in (2, 1, 3):
-        give = part(w_x, (rep + by) % 4, 4)
-        got = turn(give, by)
+        got = turn(gives[by - 1], by)
         w_sum = w_sum + got * (1.0 - inner_rate * decay_rate)
-
     w_other = swap(weight, "tp", 1)
     h_other = swap(other, "tp", 1)
-    own = jnp.dot(mine, weight, preferred_element_type=f32)
-    pair_sum = (own + jnp.dot(h_other, w_other, preferred_element_type=f32)).astype(bf16)
+    own = jnp.dot(mine, weight, preferred_element_type=f32).astype(bf16)
+    pair_sum = (own.astype(f32) + jnp.dot(h_other, w_other, preferred_element_type=f32)).astype(bf16)
     parts = spread(pair_sum.reshape(8, half // 8, cols), "tp", CHIPS)
     wide = residual_copies(parts, target, core * 8 + chip)
     res = spread(wide, "tp", CHIPS).reshape(half, cols)
@@ -122,14 +132,19 @@
     moment_one = beta_one * first_moment[0] + (1.0 - beta_one) * grad
     moment_two = beta_two * second_moment[0] + (1.0 - beta_two) * grad * grad
     step_dir = (moment_one / corr_one / (jnp.sqrt(moment_two / corr_two) + adam_eps)).astype(bf16)
-    steps = spread(step_dir.reshape(16, 32, cols), "rep")
-    updated = w_sum - inner_rate * jnp.sum(steps.astype(f32), axis=0)
+    steps = spread(step_dir.reshape(4, 128, cols), "rep", ROWS)
+    step_sum = jnp.sum(steps.astype(f32), axis=0)
+    steps = spread(step_sum.astype(bf16).reshape(4, 32, cols), "rep", COLUMNS)
+    step_sum = jnp.sum(steps.astype(f32), axis=0)
+    updated = w_sum - inner_rate * step_sum
     anchor_rows = anchor[0]
     delta = anchor_rows - updated / 16.0
     momentum_new = outer_mu * outer_momentum[0] + delta
     piece = (anchor_rows - outer_rate * (delta + outer_mu * momentum_new)).astype(bf16)
-    wide = jnp.broadcast_to(piece[None], (16,) + piece.shape)
-    fragment = spread(wide, "rep").reshape(512, cols)
+    wide = jnp.broadcast_to(piece[None], (4,) + piece.shape)
+    piece = spread(wide, "rep", COLUMNS).reshape(128, cols)
+    wide = jnp.broadcast_to(piece[None], (4,) + piece.shape)
+    fragment = spread(wide, "rep", ROWS).reshape(512, cols)
     return (fragment, momentum_new[None])
 
 

time: 197 us -> 177 us (0.90)
  waiting for transfers between devices: 71.1 us -> 49 us
  matrix products: 11.4 us -> 14.5 us
  local copies, waits for them, and re-layouts: 8.02 us -> 5.54 us
  other arithmetic: 4.6 us -> 6.83 us
    ppermute x5, waiting for transfers between devices: 37 us -> 2.51 us  [swap(): return lax.ppermute(x, axis, [(i, i ^ mask) for i in range(16)])]
    all_to_all x2 -> x3, waiting for transfers between devices: 25.6 us -> 37.9 us  [spread(): return lax.all_to_all(x, axis, 0, 0, axis_index_groups=groups)]
    all_to_all x2 -> x3, starting transfers between devices: 16.1 us -> 18.2 us  [spread(): return lax.all_to_all(x, axis, 0, 0, axis_index_groups=groups)]
    reduce_sum x1 -> x2, other arithmetic: 0.19 us -> 2.22 us  [local(): step_sum = jnp.sum(steps.astype(f32), axis=0)]
    unnamed x15 -> x11, local copies, waits for them, and re-layouts: 4.33 us -> 2.56 us
    all_to_all x2 -> x3, blocking collectives: 62.3 us -> 61.9 us  [spread(): return lax.all_to_all(x, axis, 0, 0, axis_index_groups=groups)]
  transfers between devices with their start and end apart: 10 -> 11, of which waited for: 7 -> 7; matrix products, arithmetic and copies ran while one was open for 5% -> 10% of each run, Pallas kernels for 1% -> 2%
where the time goes in v2:
time: 177 us; the launch traced here: 176 us
  blocking collectives  61.9 us (35%)
  waiting for transfers between devices  49 us (28%)
  starting transfers between devices  32 us (18%)
  matrix products  14.5 us (8%)
  other arithmetic  6.83 us (4%)
  local copies, waits for them, and re-layouts  5.54 us (3%)
  Pallas kernels  5.45 us (3%)
    all_to_all x3, blocking collectives, spread(): return lax.all_to_all(x, axis, 0, 0, axis_index_groups=groups)  61.9 us
    all_to_all x3, waiting for transfers between devices, spread(): return lax.all_to_all(x, axis, 0, 0, axis_index_groups=groups)  37.9 us
    all_to_all x3, starting transfers between devices, spread(): return lax.all_to_all(x, axis, 0, 0, axis_index_groups=groups)  18.2 us
    ppermute x3, starting transfers between devices, turn(): lax.ppermute(x, 'rep', [(i, i // 4 * 4 + (i + by) % 4) for i in range(16)])  10.1 us
    ppermute x3, waiting for transfers between devices, turn(): lax.ppermute(x, 'rep', [(i, i // 4 * 4 + (i + by) % 4) for i in range(16)])  8.65 us
    dot_general x1, matrix products, local(): lax.dot_general(other, res_other, dims, preferred_element_type=f32)  5.04 us
    dot_general x1, matrix products, local(): jnp.dot(h_other, w_other, preferred_element_type=f32)  4.14 us
    ppermute x5, starting transfers between devices, swap(): return lax.ppermute(x, axis, [(i, i ^ mask) for i in range(16)])  3.7 us
  transfers between devices with their start and end apart: 11, of which 7 were waited for; matrix products, arithmetic and copies ran while one was open for 10% of the time, Pallas kernels for 2%

profile of v2, /device:TPU:8, one launch (start us, length us, event | category | flops | bytes accessed | tf_op | source)
XLA Modules:
  0.0 176.1 jit_solution(9108813696806467665)
XLA Ops:
  0.6 0.0 copy-start
  0.7 1.6 copy-done
  2.2 0.1 constant_dynamic-slice_fusion
  2.3 0.1 collective-permute-start.5
  2.4 0.5 collective-permute-start.6
  2.9 2.5 %fusion.9 = bf16[1024,1024]{1,0:T(8,128)(2,1)S(1)} fusion(bf16[2048,512]{1,0:T(8,128)(2,1)S(1)} %copy-done, s32[]{:T(128)S(6)} %select_n.52, bf16[1,512,1024]{2,1,0:T(8,128)(2,1)} %param.9), kind=kOutput, calls=%fused_computation.13 | convolution fusion | flops 1073741824 | bytes 4194308 | tf_op jit(solution)/shard_map/dot_general | solution.py:121
  5.4 0.0 collective-permute-done.5
  5.4 1.3 collective-permute-done.6
  6.7 4.1 %add_convert_fusion = bf16[1024,1024]{1,0:T(8,128)(2,1)} fusion(bf16[1024,512]{1,0:T(8,128)(2,1)} %collective-permute-done.5, bf16[512,1024]{1,0:T(8,128)(2,1)} %collective-permute-done.6, bf16[1024,1024]{1,0:T(8,128)(2,1)S(1)} %fusion.9), kind=kOutput, calls=%fused_computation | convolution fusion | flops 1076887552 | bytes 6291456 | tf_op jit(solution)/shard_map/dot_general | solution.py:122
  10.8 6.4 %all-to-all-start = ((bf16[8,128,1024]{2,1,0:T(8,128)(2,1)}), bf16[8,128,1024]{2,1,0:T(8,128)(2,1)}, u32[]{:S(2)}, u32[]{:S(2)}) async-start(bf16[8,128,1024]{2,1,0:T(8,128)(2,1)} %bitcast.49), calls=%async_computation | async-start | bytes 4194304 | tf_op jit(solution)/shard_map/all_to_all | solution.py:26
  17.2 25.6 %all-to-all-done.parts_ref = bf16[8,128,1024]{2,1,0:T(8,128)(2,1)} async-done(((bf16[8,128,1024]{2,1,0:T(8,128)(2,1)}), bf16[8,128,1024]{2,1,0:T(8,128)(2,1)}, u32[]{:S(2)}, u32[]{:S(2)}) %all-to-all-start) | async-done | bytes 2097184 | tf_op jit(solution)/shard_map/all_to_all | solution.py:26
  42.8 2.8 %residual.1 = bf16[8,128,1024]{2,1,0:T(8,128)(2,1)} custom-call(s32[1]{0:T(128)} %bitcast.6.at_ref, bf16[8,128,1024]{2,1,0:T(8,128)(2,1)} %all-to-all-done.parts_ref, bf16[2048,1024]{1,0:T(8,128)(2,1)} %goal_ref.1), custom_call_target="tpu_custom_call" | custom-call | flops 1048576 | bytes 4194304 | tf_op jit(solution)/shard_map/residual/pallas_call | solution.py:54
  45.5 31.0 %all_to_all.30 = bf16[8,128,1024]{2,1,0:T(8,128)(2,1)} all-to-all(bf16[8,128,1024]{2,1,0:T(8,128)(2,1)} %residual.1), channel_id=1, replica_groups={{0,2,4,6,8,10,12,14},{1,3,5,7,9,11,13,15},{16,18,20,22,24,26,28,30},{17..., dimensions={0} | all-to-all | bytes 4194304 | tf_op jit(solution)/shard_map/all_to_all | solution.py:26
  76.5 0.0 collective-permute-start.7
  76.5 1.9 %dynamic-slice_bitcast_fusion = bf16[256,1024]{1,0:T(8,128)(2,1)} fusion(bf16[1,512,1024]{2,1,0:T(8,128)(2,1)} %param.9, s32[]{:T(128)S(6)} %select_n.49), kind=kLoop, calls=%fused_computation.16 | loop fusion | bytes 1048580 | tf_op jit(solution)/shard_map/dynamic_slice | solution.py:39
  78.4 2.4 %collective-permute-start = (bf16[256,1024]{1,0:T(8,128)(2,1)}, bf16[256,1024]{1,0:T(8,128)(2,1)}, u32[]{:S(2)}, u32[]{:S(2)}) collective-permute-start(bf16[256,1024]{1,0:T(8,128)(2,1)} %dynamic-slice_bitcast_fusion), channel_id=1, source_target_pairs={{0,192},{16,208},{32,224},{48,240},{64,128},{80,144},{96,160},{112... | collective-permute-start | bytes 1572872 | tf_op jit(solution)/shard_map/ppermute | solution.py:30
  80.8 2.9 %fusion.7 = f32[512,1024]{1,0:T(8,128)S(1)} fusion(bf16[1024,1024]{1,0:T(8,128)(2,1)} %bitcast.9, bf16[2048,512]{1,0:T(8,128)(2,1)S(1)} %copy-done, s32[]{:T(128)S(6)} %select_n.52), kind=kOutput, calls=%fused_computation.11 | convolution fusion | flops 1073741824 | bytes 5242884 | tf_op jit(solution)/shard_map/dot_general | solution.py:130
  83.7 0.0 collective-permute-done.7
  83.7 0.0 copy-done.3
  83.7 0.0 copy-done.4
  83.7 5.0 %fusion.6 = bf16[512,1024]{1,0:T(8,128)(2,1)} fusion(f32[1,512,1024]{2,1,0:T(8,128)S(1)} %copy-done.3, f32[512,1024]{1,0:T(8,128)S(1)} %fusion.7, f32[1,512,1024]{2,1,0:T(8,128)S(1)} %copy-done.4, bf16[1024,512]{1,0:T(8,128)(2,1)S(1)} %constant_dynamic-slice_fusion, bf16[1024,1024]{1,0:T(8,128)(2,1)} %collective-permute-done.7), kind=kOutput, calls=%fused_computation.9 | convolution fusion | flops 1080557568 | bytes 10485760 | tf_op jit(solution)/shard_map/dot_general | solution.py:131
  88.7 4.3 %all-to-all-start.2 = ((bf16[4,128,1024]{2,1,0:T(8,128)(2,1)}), bf16[4,128,1024]{2,1,0:T(8,128)(2,1)}, u32[]{:S(2)}, u32[]{:S(2)}) async-start(bf16[4,128,1024]{2,1,0:T(8,128)(2,1)} %bitcast.51), calls=%async_computation.2 | async-start | bytes 2097152 | tf_op jit(solution)/shard_map/all_to_all | solution.py:26
  93.1 1.2 collective-permute-done
  94.3 1.4 convert_add_fusion.x_ref
  95.6 0.0 copy-start.1
  95.7 0.9 constant_dynamic-slice_fusion.1
  96.6 0.7 collective-permute-start.1
  97.3 12.3 %all-to-all-done.2 = bf16[4,128,1024]{2,1,0:T(8,128)(2,1)} async-done(((bf16[4,128,1024]{2,1,0:T(8,128)(2,1)}), bf16[4,128,1024]{2,1,0:T(8,128)(2,1)}, u32[]{:S(2)}, u32[]{:S(2)}) %all-to-all-start.2) | async-done | bytes 1048608 | tf_op jit(solution)/shard_map/all_to_all | solution.py:26
  109.6 2.2 %reduce_sum.21 = bf16[128,1024]{1,0:T(8,128)(2,1)} reduce(bf16[4,128,1024]{2,1,0:T(8,128)(2,1)} %all-to-all-done.2, bf16[]{:T(256)} %constant.109.clone.1), dimensions={0}, to_apply=%region_0.1 | reduce | flops 393216 | bytes 1310722 | tf_op jit(solution)/shard_map/reduce_sum | solution.py:136
  111.8 7.6 %all-to-all-start.3 = ((bf16[4,32,1024]{2,1,0:T(8,128)(2,1)}), bf16[4,32,1024]{2,1,0:T(8,128)(2,1)S(1)}, u32[]{:S(2)}, u32[]{:S(2)}) async-start(bf16[4,32,1024]{2,1,0:T(8,128)(2,1)} %bitcast.12), calls=%async_computation.3 | async-start | bytes 524288 | tf_op jit(solution)/shard_map/all_to_all | solution.py:26
  119.3 0.6 pad_add_fusion.at_ref
  119.9 0.0 collective-permute-done.1.got_ref
  119.9 0.0 copy-done.1
  119.9 2.7 %summed_parts.1 = (f32[32,1024]{1,0:T(8,128)}, f32[32,1024]{1,0:T(8,128)}, f32[32,1024]{1,0:T(8,128)}, f32[32,1024]{1,0:T(8,128)}) custom-call(s32[2]{0:T(128)} %pad_add_fusion.at_ref, f32[256,1024]{1,0:T(8,128)} %copy-done.1, f32[128,1024]{1,0:T(8,128)} %collective-permute-done.1.got_ref), custom_call_target="tpu_custom_call" | custom-call | flops 131072 | bytes 1572864 | tf_op jit(solution)/shard_map/summed_parts/pallas_call | solution.py:85
  122.6 5.9 %collective-permute-start.2 = (f32[32,1024]{1,0:T(8,128)}, f32[32,1024]{1,0:T(8,128)S(1)}, u32[]{:S(2)}, u32[]{:S(2)}) collective-permute-start(f32[32,1024]{1,0:T(8,128)} %get-tuple-element.7), channel_id=1, source_target_pairs={{0,32},{16,48},{32,0},{48,16},{64,96},{80,112},{96,64},{112,80},{1... | collective-permute-start | bytes 393224 | tf_op jit(solution)/shard_map/ppermute | solution.py:34
  128.6 0.6 collective-permute-start.3
  129.1 3.6 %collective-permute-start.4 = (f32[32,1024]{1,0:T(8,128)}, f32[32,1024]{1,0:T(8,128)S(1)}, u32[]{:S(2)}, u32[]{:S(2)}) collective-permute-start(f32[32,1024]{1,0:T(8,128)} %get-tuple-element.9), channel_id=1, source_target_pairs={{0,48},{16,0},{32,16},{48,32},{64,112},{80,64},{96,80},{112,96},{1... | collective-permute-start | bytes 393224 | tf_op jit(solution)/shard_map/ppermute | solution.py:34
  132.7 0.0 all-to-all-done.3
  132.7 3.4 %collective-permute-done.2 = f32[32,1024]{1,0:T(8,128)S(1)} collective-permute-done((f32[32,1024]{1,0:T(8,128)}, f32[32,1024]{1,0:T(8,128)S(1)}, u32[]{:S(2)}, u32[]{:S(2)}) %collective-permute-start.2) | collective-permute-done | bytes 131104 | tf_op jit(solution)/shard_map/ppermute | solution.py:34
  136.1 2.9 %collective-permute-done.3 = f32[32,1024]{1,0:T(8,128)S(1)} collective-permute-done((f32[32,1024]{1,0:T(8,128)}, f32[32,1024]{1,0:T(8,128)S(1)}, u32[]{:S(2)}, u32[]{:S(2)}) %collective-permute-start.3) | collective-permute-done | bytes 131104 | tf_op jit(solution)/shard_map/ppermute | solution.py:34
  139.0 2.4 %collective-permute-done.4 = f32[32,1024]{1,0:T(8,128)S(1)} collective-permute-done((f32[32,1024]{1,0:T(8,128)}, f32[32,1024]{1,0:T(8,128)S(1)}, u32[]{:S(2)}, u32[]{:S(2)}) %collective-permute-start.4) | collective-permute-done | bytes 131104 | tf_op jit(solution)/shard_map/ppermute | solution.py:34
  141.4 0.0 copy-done.2
  141.4 1.7 fusion.12
  143.1 0.9 fusion.11
  144.1 14.4 %all_to_all.31 = bf16[4,32,1024]{2,1,0:T(8,128)(2,1)S(1)} all-to-all(bf16[4,32,1024]{2,1,0:T(8,128)(2,1)S(1)} %broadcast_in_dim.16), channel_id=1, replica_groups={{0,16,32,48},{64,80,96,112},{128,144,160,176},{192,208,224,240},{1,17,3..., dimensions={0} | all-to-all | bytes 524288 | tf_op jit(solution)/shard_map/all_to_all | solution.py:26
  158.4 0.1 broadcast_in_dim.18
  158.6 16.6 %all_to_all.32 = bf16[4,128,1024]{2,1,0:T(8,128)(2,1)S(1)} all-to-all(bf16[4,128,1024]{2,1,0:T(8,128)(2,1)S(1)} %broadcast_in_dim.18), channel_id=1, replica_groups={{0,64,128,192},{16,80,144,208},{32,96,160,224},{48,112,176,240},{1,65,1..., dimensions={0} | all-to-all | bytes 2097152 | tf_op jit(solution)/shard_map/all_to_all | solution.py:26
  175.1 1.0 copy.10
  (5 shorter events, 0.1 us)
Async XLA Ops:
  0.6 1.6 copy-start
  2.3 3.1 %collective-permute-start.5 = (bf16[1024,512]{1,0:T(8,128)(2,1)S(1)}, bf16[1024,512]{1,0:T(8,128)(2,1)}, u32[]{:S(2)}, u32[]{:S(2)}) collective-permute-start(bf16[1024,512]{1,0:T(8,128)(2,1)S(1)} %constant_dynamic-slice_fusion), channel_id=1, source_target_pairs={{0,1},{1,0},{2,3},{3,2},{4,5},{5,4},{6,7},{7,6},{8,9},{9,8},{10,11... | collective-permute-start | bytes 3145736 | tf_op jit(solution)/shard_map/ppermute | solution.py:30
  2.4 4.3 %collective-permute-start.6 = (bf16[512,1024]{1,0:T(8,128)(2,1)}, bf16[512,1024]{1,0:T(8,128)(2,1)}, u32[]{:S(2)}, u32[]{:S(2)}) collective-permute-start(bf16[512,1024]{1,0:T(8,128)(2,1)} %bitcast.7), channel_id=1, source_target_pairs={{0,1},{1,0},{2,3},{3,2},{4,5},{5,4},{6,7},{7,6},{8,9},{9,8},{10,11... | collective-permute-start | bytes 3145736 | tf_op jit(solution)/shard_map/ppermute | solution.py:30
  10.8 31.9 %all-to-all-start = ((bf16[8,128,1024]{2,1,0:T(8,128)(2,1)}), bf16[8,128,1024]{2,1,0:T(8,128)(2,1)}, u32[]{:S(2)}, u32[]{:S(2)}) async-start(bf16[8,128,1024]{2,1,0:T(8,128)(2,1)} %bitcast.49), calls=%async_computation | async-start | bytes 4194304 | tf_op jit(solution)/shard_map/all_to_all | solution.py:26
  76.5 7.1 %collective-permute-start.7 = (bf16[1024,1024]{1,0:T(8,128)(2,1)}, bf16[1024,1024]{1,0:T(8,128)(2,1)}, u32[]{:S(2)}, u32[]{:S(2)}) collective-permute-start(bf16[1024,1024]{1,0:T(8,128)(2,1)} %bitcast.9), channel_id=1, source_target_pairs={{0,1},{1,0},{2,3},{3,2},{4,5},{5,4},{6,7},{7,6},{8,9},{9,8},{10,11... | collective-permute-start | bytes 6291464 | tf_op jit(solution)/shard_map/ppermute | solution.py:30
  78.4 5.3 %copy-start.3 = (f32[1,512,1024]{2,1,0:T(8,128)S(1)}, f32[1,512,1024]{2,1,0:T(8,128)}, u32[]{:S(2)}) copy-start(f32[1,512,1024]{2,1,0:T(8,128)} %param.11) | copy-start | bytes 6291460
  78.4 5.3 %copy-start.4 = (f32[1,512,1024]{2,1,0:T(8,128)S(1)}, f32[1,512,1024]{2,1,0:T(8,128)}, u32[]{:S(2)}) copy-start(f32[1,512,1024]{2,1,0:T(8,128)} %param.10) | copy-start | bytes 6291460
  78.4 15.9 %collective-permute-start = (bf16[256,1024]{1,0:T(8,128)(2,1)}, bf16[256,1024]{1,0:T(8,128)(2,1)}, u32[]{:S(2)}, u32[]{:S(2)}) collective-permute-start(bf16[256,1024]{1,0:T(8,128)(2,1)} %dynamic-slice_bitcast_fusion), channel_id=1, source_target_pairs={{0,192},{16,208},{32,224},{48,240},{64,128},{80,144},{96,160},{112... | collective-permute-start | bytes 1572872 | tf_op jit(solution)/shard_map/ppermute | solution.py:30
  88.7 20.8 %all-to-all-start.2 = ((bf16[4,128,1024]{2,1,0:T(8,128)(2,1)}), bf16[4,128,1024]{2,1,0:T(8,128)(2,1)}, u32[]{:S(2)}, u32[]{:S(2)}) async-start(bf16[4,128,1024]{2,1,0:T(8,128)(2,1)} %bitcast.51), calls=%async_computation.2 | async-start | bytes 2097152 | tf_op jit(solution)/shard_map/all_to_all | solution.py:26
  95.6 24.3 %copy-start.1 = (f32[256,1024]{1,0:T(8,128)}, f32[256,1024]{1,0:T(8,128)S(1)}, u32[]{:S(2)}) copy-start(f32[256,1024]{1,0:T(8,128)S(1)} %convert_add_fusion.x_ref) | copy-start | bytes 3145732
  96.6 44.8 %copy-start.2 = (f32[1,32,1024]{2,1,0:T(8,128)S(1)}, f32[1,32,1024]{2,1,0:T(8,128)}, u32[]{:S(2)}) copy-start(f32[1,32,1024]{2,1,0:T(8,128)} %param.12) | copy-start | bytes 393220
  96.6 23.4 %collective-permute-start.1 = (f32[128,1024]{1,0:T(8,128)}, f32[128,1024]{1,0:T(8,128)}, u32[]{:S(2)}, u32[]{:S(2)}) collective-permute-start(f32[128,1024]{1,0:T(8,128)} %constant_dynamic-slice_fusion.1), channel_id=1, source_target_pairs={{0,64},{16,80},{32,96},{48,112},{64,0},{80,16},{96,32},{112,48},{1... | collective-permute-start | bytes 1572872 | tf_op jit(solution)/shard_map/ppermute | solution.py:30
  111.8 20.9 %all-to-all-start.3 = ((bf16[4,32,1024]{2,1,0:T(8,128)(2,1)}), bf16[4,32,1024]{2,1,0:T(8,128)(2,1)S(1)}, u32[]{:S(2)}, u32[]{:S(2)}) async-start(bf16[4,32,1024]{2,1,0:T(8,128)(2,1)} %bitcast.12), calls=%async_computation.3 | async-start | bytes 524288 | tf_op jit(solution)/shard_map/all_to_all | solution.py:26
  122.6 13.5 %collective-permute-start.2 = (f32[32,1024]{1,0:T(8,128)}, f32[32,1024]{1,0:T(8,128)S(1)}, u32[]{:S(2)}, u32[]{:S(2)}) collective-permute-start(f32[32,1024]{1,0:T(8,128)} %get-tuple-element.7), channel_id=1, source_target_pairs={{0,32},{16,48},{32,0},{48,16},{64,96},{80,112},{96,64},{112,80},{1... | collective-permute-start | bytes 393224 | tf_op jit(solution)/shard_map/ppermute | solution.py:34
  128.6 10.4 %collective-permute-start.3 = (f32[32,1024]{1,0:T(8,128)}, f32[32,1024]{1,0:T(8,128)S(1)}, u32[]{:S(2)}, u32[]{:S(2)}) collective-permute-start(f32[32,1024]{1,0:T(8,128)} %get-tuple-element.8), channel_id=1, source_target_pairs={{0,16},{16,32},{32,48},{48,0},{64,80},{80,96},{96,112},{112,64},{1... | collective-permute-start | bytes 393224 | tf_op jit(solution)/shard_map/ppermute | solution.py:34
  129.1 12.3 %collective-permute-start.4 = (f32[32,1024]{1,0:T(8,128)}, f32[32,1024]{1,0:T(8,128)S(1)}, u32[]{:S(2)}, u32[]{:S(2)}) collective-permute-start(f32[32,1024]{1,0:T(8,128)} %get-tuple-element.9), channel_id=1, source_target_pairs={{0,48},{16,0},{32,16},{48,32},{64,112},{80,64},{96,80},{112,96},{1... | collective-permute-start | bytes 393224 | tf_op jit(solution)/shard_map/ppermute | solution.py:34

commit v3 on v2

--- a/solution.py
+++ b/solution.py
@@ -113,9 +113,10 @@
     give = part(w_x, 1 - rep // 4 % 2, 2)
     got = swap(give, "rep", 4)
     w_sum, *gives = summed_parts(w_x, got, rep // 4 % 2, rep % 4, 1.0 - inner_rate * decay_rate)
+    turned = []
     for by in (2, 1, 3):
-        got = turn(gives[by - 1], by)
-        w_sum = w_sum + got * (1.0 - inner_rate * decay_rate)
+        turned.append(turn(gives[by - 1], by))
+    w_sum = lax.optimization_barrier(w_sum + (turned[0] + turned[1] + turned[2]) * (1.0 - inner_rate * decay_rate))
     w_other = swap(weight, "tp", 1)
     h_other = swap(other, "tp", 1)
     own = jnp.dot(mine, weight, preferred_element_type=f32).astype(bf16)

time: 177 us -> 177 us (level)
  no operation moved by 1% of the time
where the time goes in v3:
time: 177 us; the launch traced here: 176 us
  blocking collectives  61.9 us (35%)
  waiting for transfers between devices  48.9 us (28%)
  starting transfers between devices  32.1 us (18%)
  matrix products  14.7 us (8%)
  other arithmetic  6.76 us (4%)
  local copies, waits for them, and re-layouts  5.55 us (3%)
  Pallas kernels  5.45 us (3%)
    all_to_all x3, blocking collectives, spread(): return lax.all_to_all(x, axis, 0, 0, axis_index_groups=groups)  61.9 us
    all_to_all x3, waiting for transfers between devices, spread(): return lax.all_to_all(x, axis, 0, 0, axis_index_groups=groups)  37.8 us
    all_to_all x3, starting transfers between devices, spread(): return lax.all_to_all(x, axis, 0, 0, axis_index_groups=groups)  18.2 us
    ppermute x3, starting transfers between devices, turn(): lax.ppermute(x, 'rep', [(i, i // 4 * 4 + (i + by) % 4) for i in range(16)])  10.1 us
    ppermute x3, waiting for transfers between devices, turn(): lax.ppermute(x, 'rep', [(i, i // 4 * 4 + (i + by) % 4) for i in range(16)])  8.69 us
    dot_general x1, matrix products, local(): lax.dot_general(other, res_other, dims, preferred_element_type=f32)  5.07 us
    dot_general x1, matrix products, local(): jnp.dot(h_other, w_other, preferred_element_type=f32)  4.14 us
    ppermute x5, starting transfers between devices, swap(): return lax.ppermute(x, axis, [(i, i ^ mask) for i in range(16)])  3.86 us
  transfers between devices with their start and end apart: 11, of which 7 were waited for; matrix products, arithmetic and copies ran while one was open for 10% of the time, Pallas kernels for 2%

profile of v3, /device:TPU:8, one launch (start us, length us, event | category | flops | bytes accessed | tf_op | source)
XLA Modules:
  0.0 176.2 jit_solution(2984376416756872793)
XLA Ops:
  0.6 0.0 copy-start
  0.7 1.6 copy-done
  2.2 0.1 constant_dynamic-slice_fusion
  2.3 0.1 collective-permute-start.5
  2.4 0.5 collective-permute-start.6
  2.9 2.5 %fusion.9 = bf16[1024,1024]{1,0:T(8,128)(2,1)S(1)} fusion(bf16[2048,512]{1,0:T(8,128)(2,1)S(1)} %copy-done, s32[]{:T(128)S(6)} %select_n.52, bf16[1,512,1024]{2,1,0:T(8,128)(2,1)} %param.9), kind=kOutput, calls=%fused_computation.13 | convolution fusion | flops 1073741824 | bytes 4194308 | tf_op jit(solution)/shard_map/dot_general | solution.py:122
  5.4 0.0 collective-permute-done.5
  5.4 1.3 collective-permute-done.6
  6.7 4.1 %add_convert_fusion = bf16[1024,1024]{1,0:T(8,128)(2,1)} fusion(bf16[1024,512]{1,0:T(8,128)(2,1)} %collective-permute-done.5, bf16[512,1024]{1,0:T(8,128)(2,1)} %collective-permute-done.6, bf16[1024,1024]{1,0:T(8,128)(2,1)S(1)} %fusion.9), kind=kOutput, calls=%fused_computation | convolution fusion | flops 1076887552 | bytes 6291456 | tf_op jit(solution)/shard_map/dot_general | solution.py:123
  10.8 6.4 %all-to-all-start = ((bf16[8,128,1024]{2,1,0:T(8,128)(2,1)}), bf16[8,128,1024]{2,1,0:T(8,128)(2,1)}, u32[]{:S(2)}, u32[]{:S(2)}) async-start(bf16[8,128,1024]{2,1,0:T(8,128)(2,1)} %bitcast.52), calls=%async_computation | async-start | bytes 4194304 | tf_op jit(solution)/shard_map/all_to_all | solution.py:26
  17.2 25.6 %all-to-all-done.parts_ref = bf16[8,128,1024]{2,1,0:T(8,128)(2,1)} async-done(((bf16[8,128,1024]{2,1,0:T(8,128)(2,1)}), bf16[8,128,1024]{2,1,0:T(8,128)(2,1)}, u32[]{:S(2)}, u32[]{:S(2)}) %all-to-all-start) | async-done | bytes 2097184 | tf_op jit(solution)/shard_map/all_to_all | solution.py:26
  42.8 2.8 %residual.1 = bf16[8,128,1024]{2,1,0:T(8,128)(2,1)} custom-call(s32[1]{0:T(128)} %bitcast.6.at_ref, bf16[8,128,1024]{2,1,0:T(8,128)(2,1)} %all-to-all-done.parts_ref, bf16[2048,1024]{1,0:T(8,128)(2,1)} %goal_ref.1), custom_call_target="tpu_custom_call" | custom-call | flops 1048576 | bytes 4194304 | tf_op jit(solution)/shard_map/residual/pallas_call | solution.py:54
  45.5 31.0 %all_to_all.30 = bf16[8,128,1024]{2,1,0:T(8,128)(2,1)} all-to-all(bf16[8,128,1024]{2,1,0:T(8,128)(2,1)} %residual.1), channel_id=1, replica_groups={{0,2,4,6,8,10,12,14},{1,3,5,7,9,11,13,15},{16,18,20,22,24,26,28,30},{17..., dimensions={0} | all-to-all | bytes 4194304 | tf_op jit(solution)/shard_map/all_to_all | solution.py:26
  76.5 0.0 collective-permute-start.7
  76.5 1.9 %dynamic-slice_bitcast_fusion = bf16[256,1024]{1,0:T(8,128)(2,1)} fusion(bf16[1,512,1024]{2,1,0:T(8,128)(2,1)} %param.9, s32[]{:T(128)S(6)} %select_n.49), kind=kLoop, calls=%fused_computation.16 | loop fusion | bytes 1048580 | tf_op jit(solution)/shard_map/dynamic_slice | solution.py:39
  78.4 2.4 %collective-permute-start = (bf16[256,1024]{1,0:T(8,128)(2,1)}, bf16[256,1024]{1,0:T(8,128)(2,1)}, u32[]{:S(2)}, u32[]{:S(2)}) collective-permute-start(bf16[256,1024]{1,0:T(8,128)(2,1)} %dynamic-slice_bitcast_fusion), channel_id=1, source_target_pairs={{0,192},{16,208},{32,224},{48,240},{64,128},{80,144},{96,160},{112... | collective-permute-start | bytes 1572872 | tf_op jit(solution)/shard_map/ppermute | solution.py:30
  80.8 3.0 %fusion.7 = f32[512,1024]{1,0:T(8,128)S(1)} fusion(bf16[1024,1024]{1,0:T(8,128)(2,1)} %bitcast.9, bf16[2048,512]{1,0:T(8,128)(2,1)S(1)} %copy-done, s32[]{:T(128)S(6)} %select_n.52), kind=kOutput, calls=%fused_computation.11 | convolution fusion | flops 1073741824 | bytes 5242884 | tf_op jit(solution)/shard_map/dot_general | solution.py:131
  83.8 0.0 collective-permute-done.7
  83.8 0.0 copy-done.3
  83.8 0.0 copy-done.4
  83.8 5.1 %fusion.6 = bf16[512,1024]{1,0:T(8,128)(2,1)} fusion(f32[1,512,1024]{2,1,0:T(8,128)S(1)} %copy-done.3, f32[512,1024]{1,0:T(8,128)S(1)} %fusion.7, f32[1,512,1024]{2,1,0:T(8,128)S(1)} %copy-done.4, bf16[1024,512]{1,0:T(8,128)(2,1)S(1)} %constant_dynamic-slice_fusion, bf16[1024,1024]{1,0:T(8,128)(2,1)} %collective-permute-done.7), kind=kOutput, calls=%fused_computation.9 | convolution fusion | flops 1080557568 | bytes 10485760 | tf_op jit(solution)/shard_map/dot_general | solution.py:132
  88.9 4.2 %all-to-all-start.2 = ((bf16[4,128,1024]{2,1,0:T(8,128)(2,1)}), bf16[4,128,1024]{2,1,0:T(8,128)(2,1)}, u32[]{:S(2)}, u32[]{:S(2)}) async-start(bf16[4,128,1024]{2,1,0:T(8,128)(2,1)} %bitcast.54), calls=%async_computation.2 | async-start | bytes 2097152 | tf_op jit(solution)/shard_map/all_to_all | solution.py:26
  93.2 1.1 collective-permute-done
  94.3 1.4 convert_add_fusion.x_ref
  95.6 0.0 copy-start.1
  95.7 0.9 constant_dynamic-slice_fusion.1
  96.6 0.9 collective-permute-start.1
  97.4 12.3 %all-to-all-done.2 = bf16[4,128,1024]{2,1,0:T(8,128)(2,1)} async-done(((bf16[4,128,1024]{2,1,0:T(8,128)(2,1)}), bf16[4,128,1024]{2,1,0:T(8,128)(2,1)}, u32[]{:S(2)}, u32[]{:S(2)}) %all-to-all-start.2) | async-done | bytes 1048608 | tf_op jit(solution)/shard_map/all_to_all | solution.py:26
  109.7 2.2 %reduce_sum.21 = bf16[128,1024]{1,0:T(8,128)(2,1)} reduce(bf16[4,128,1024]{2,1,0:T(8,128)(2,1)} %all-to-all-done.2, bf16[]{:T(256)} %constant.109.clone.1), dimensions={0}, to_apply=%region_0.1 | reduce | flops 393216 | bytes 1310722 | tf_op jit(solution)/shard_map/reduce_sum | solution.py:137
  111.9 7.6 %all-to-all-start.3 = ((bf16[4,32,1024]{2,1,0:T(8,128)(2,1)}), bf16[4,32,1024]{2,1,0:T(8,128)(2,1)S(1)}, u32[]{:S(2)}, u32[]{:S(2)}) async-start(bf16[4,32,1024]{2,1,0:T(8,128)(2,1)} %bitcast.12), calls=%async_computation.3 | async-start | bytes 524288 | tf_op jit(solution)/shard_map/all_to_all | solution.py:26
  119.5 0.6 pad_add_fusion.at_ref
  120.1 0.0 collective-permute-done.1.got_ref
  120.1 0.0 copy-done.1
  120.1 2.7 %summed_parts.1 = (f32[32,1024]{1,0:T(8,128)}, f32[32,1024]{1,0:T(8,128)}, f32[32,1024]{1,0:T(8,128)}, f32[32,1024]{1,0:T(8,128)}) custom-call(s32[2]{0:T(128)} %pad_add_fusion.at_ref, f32[256,1024]{1,0:T(8,128)} %copy-done.1, f32[128,1024]{1,0:T(8,128)} %collective-permute-done.1.got_ref), custom_call_target="tpu_custom_call" | custom-call | flops 131072 | bytes 1572864 | tf_op jit(solution)/shard_map/summed_parts/pallas_call | solution.py:85
  122.8 5.9 %collective-permute-start.2 = (f32[32,1024]{1,0:T(8,128)}, f32[32,1024]{1,0:T(8,128)S(1)}, u32[]{:S(2)}, u32[]{:S(2)}) collective-permute-start(f32[32,1024]{1,0:T(8,128)} %get-tuple-element.7), channel_id=1, source_target_pairs={{0,32},{16,48},{32,0},{48,16},{64,96},{80,112},{96,64},{112,80},{1... | collective-permute-start | bytes 393224 | tf_op jit(solution)/shard_map/ppermute | solution.py:34
  128.7 0.6 collective-permute-start.3
  129.3 3.6 %collective-permute-start.4 = (f32[32,1024]{1,0:T(8,128)}, f32[32,1024]{1,0:T(8,128)S(1)}, u32[]{:S(2)}, u32[]{:S(2)}) collective-permute-start(f32[32,1024]{1,0:T(8,128)} %get-tuple-element.9), channel_id=1, source_target_pairs={{0,48},{16,0},{32,16},{48,32},{64,112},{80,64},{96,80},{112,96},{1... | collective-permute-start | bytes 393224 | tf_op jit(solution)/shard_map/ppermute | solution.py:34
  132.9 3.5 %collective-permute-done.2 = f32[32,1024]{1,0:T(8,128)S(1)} collective-permute-done((f32[32,1024]{1,0:T(8,128)}, f32[32,1024]{1,0:T(8,128)S(1)}, u32[]{:S(2)}, u32[]{:S(2)}) %collective-permute-start.2) | collective-permute-done | bytes 131104 | tf_op jit(solution)/shard_map/ppermute | solution.py:34
  136.4 2.8 %collective-permute-done.3 = f32[32,1024]{1,0:T(8,128)S(1)} collective-permute-done((f32[32,1024]{1,0:T(8,128)}, f32[32,1024]{1,0:T(8,128)S(1)}, u32[]{:S(2)}, u32[]{:S(2)}) %collective-permute-start.3) | collective-permute-done | bytes 131104 | tf_op jit(solution)/shard_map/ppermute | solution.py:34
  139.2 2.4 %collective-permute-done.4 = f32[32,1024]{1,0:T(8,128)S(1)} collective-permute-done((f32[32,1024]{1,0:T(8,128)}, f32[32,1024]{1,0:T(8,128)S(1)}, u32[]{:S(2)}, u32[]{:S(2)}) %collective-permute-start.4) | collective-permute-done | bytes 131104 | tf_op jit(solution)/shard_map/ppermute | solution.py:34
  141.5 0.9 multiply_add_fusion
  142.5 0.0 all-to-all-done.3
  142.5 0.0 copy-done.2
  142.5 1.6 fusion.12
  144.2 14.3 %all_to_all.31 = bf16[4,32,1024]{2,1,0:T(8,128)(2,1)S(1)} all-to-all(bf16[4,32,1024]{2,1,0:T(8,128)(2,1)S(1)} %broadcast_in_dim.16), channel_id=1, replica_groups={{0,16,32,48},{64,80,96,112},{128,144,160,176},{192,208,224,240},{1,17,3..., dimensions={0} | all-to-all | bytes 524288 | tf_op jit(solution)/shard_map/all_to_all | solution.py:26
  158.5 0.1 broadcast_in_dim.18
  158.7 16.6 %all_to_all.32 = bf16[4,128,1024]{2,1,0:T(8,128)(2,1)S(1)} all-to-all(bf16[4,128,1024]{2,1,0:T(8,128)(2,1)S(1)} %broadcast_in_dim.18), channel_id=1, replica_groups={{0,64,128,192},{16,80,144,208},{32,96,160,224},{48,112,176,240},{1,65,1..., dimensions={0} | all-to-all | bytes 2097152 | tf_op jit(solution)/shard_map/all_to_all | solution.py:26
  175.2 1.0 copy.10
  (5 shorter events, 0.1 us)
Async XLA Ops:
  0.6 1.6 copy-start
  2.3 3.1 %collective-permute-start.5 = (bf16[1024,512]{1,0:T(8,128)(2,1)S(1)}, bf16[1024,512]{1,0:T(8,128)(2,1)}, u32[]{:S(2)}, u32[]{:S(2)}) collective-permute-start(bf16[1024,512]{1,0:T(8,128)(2,1)S(1)} %constant_dynamic-slice_fusion), channel_id=1, source_target_pairs={{0,1},{1,0},{2,3},{3,2},{4,5},{5,4},{6,7},{7,6},{8,9},{9,8},{10,11... | collective-permute-start | bytes 3145736 | tf_op jit(solution)/shard_map/ppermute | solution.py:30
  2.4 4.3 %collective-permute-start.6 = (bf16[512,1024]{1,0:T(8,128)(2,1)}, bf16[512,1024]{1,0:T(8,128)(2,1)}, u32[]{:S(2)}, u32[]{:S(2)}) collective-permute-start(bf16[512,1024]{1,0:T(8,128)(2,1)} %bitcast.7), channel_id=1, source_target_pairs={{0,1},{1,0},{2,3},{3,2},{4,5},{5,4},{6,7},{7,6},{8,9},{9,8},{10,11... | collective-permute-start | bytes 3145736 | tf_op jit(solution)/shard_map/ppermute | solution.py:30
  10.8 31.9 %all-to-all-start = ((bf16[8,128,1024]{2,1,0:T(8,128)(2,1)}), bf16[8,128,1024]{2,1,0:T(8,128)(2,1)}, u32[]{:S(2)}, u32[]{:S(2)}) async-start(bf16[8,128,1024]{2,1,0:T(8,128)(2,1)} %bitcast.52), calls=%async_computation | async-start | bytes 4194304 | tf_op jit(solution)/shard_map/all_to_all | solution.py:26
  76.5 7.3 %collective-permute-start.7 = (bf16[1024,1024]{1,0:T(8,128)(2,1)}, bf16[1024,1024]{1,0:T(8,128)(2,1)}, u32[]{:S(2)}, u32[]{:S(2)}) collective-permute-start(bf16[1024,1024]{1,0:T(8,128)(2,1)} %bitcast.9), channel_id=1, source_target_pairs={{0,1},{1,0},{2,3},{3,2},{4,5},{5,4},{6,7},{7,6},{8,9},{9,8},{10,11... | collective-permute-start | bytes 6291464 | tf_op jit(solution)/shard_map/ppermute | solution.py:30
  78.4 15.9 %collective-permute-start = (bf16[256,1024]{1,0:T(8,128)(2,1)}, bf16[256,1024]{1,0:T(8,128)(2,1)}, u32[]{:S(2)}, u32[]{:S(2)}) collective-permute-start(bf16[256,1024]{1,0:T(8,128)(2,1)} %dynamic-slice_bitcast_fusion), channel_id=1, source_target_pairs={{0,192},{16,208},{32,224},{48,240},{64,128},{80,144},{96,160},{112... | collective-permute-start | bytes 1572872 | tf_op jit(solution)/shard_map/ppermute | solution.py:30
  80.8 3.0 %copy-start.3 = (f32[1,512,1024]{2,1,0:T(8,128)S(1)}, f32[1,512,1024]{2,1,0:T(8,128)}, u32[]{:S(2)}) copy-start(f32[1,512,1024]{2,1,0:T(8,128)} %param.11) | copy-start | bytes 6291460
  80.8 3.0 %copy-start.4 = (f32[1,512,1024]{2,1,0:T(8,128)S(1)}, f32[1,512,1024]{2,1,0:T(8,128)}, u32[]{:S(2)}) copy-start(f32[1,512,1024]{2,1,0:T(8,128)} %param.10) | copy-start | bytes 6291460
  88.9 20.8 %all-to-all-start.2 = ((bf16[4,128,1024]{2,1,0:T(8,128)(2,1)}), bf16[4,128,1024]{2,1,0:T(8,128)(2,1)}, u32[]{:S(2)}, u32[]{:S(2)}) async-start(bf16[4,128,1024]{2,1,0:T(8,128)(2,1)} %bitcast.54), calls=%async_computation.2 | async-start | bytes 2097152 | tf_op jit(solution)/shard_map/all_to_all | solution.py:26
  95.6 24.5 %copy-start.1 = (f32[256,1024]{1,0:T(8,128)}, f32[256,1024]{1,0:T(8,128)S(1)}, u32[]{:S(2)}) copy-start(f32[256,1024]{1,0:T(8,128)S(1)} %convert_add_fusion.x_ref) | copy-start | bytes 3145732
  96.6 23.5 %collective-permute-start.1 = (f32[128,1024]{1,0:T(8,128)}, f32[128,1024]{1,0:T(8,128)}, u32[]{:S(2)}, u32[]{:S(2)}) collective-permute-start(f32[128,1024]{1,0:T(8,128)} %constant_dynamic-slice_fusion.1), channel_id=1, source_target_pairs={{0,64},{16,80},{32,96},{48,112},{64,0},{80,16},{96,32},{112,48},{1... | collective-permute-start | bytes 1572872 | tf_op jit(solution)/shard_map/ppermute | solution.py:30
  97.4 45.1 %copy-start.2 = (f32[1,32,1024]{2,1,0:T(8,128)S(1)}, f32[1,32,1024]{2,1,0:T(8,128)}, u32[]{:S(2)}) copy-start(f32[1,32,1024]{2,1,0:T(8,128)} %param.13) | copy-start | bytes 393220
  111.9 30.6 %all-to-all-start.3 = ((bf16[4,32,1024]{2,1,0:T(8,128)(2,1)}), bf16[4,32,1024]{2,1,0:T(8,128)(2,1)S(1)}, u32[]{:S(2)}, u32[]{:S(2)}) async-start(bf16[4,32,1024]{2,1,0:T(8,128)(2,1)} %bitcast.12), calls=%async_computation.3 | async-start | bytes 524288 | tf_op jit(solution)/shard_map/all_to_all | solution.py:26
  122.8 13.6 %collective-permute-start.2 = (f32[32,1024]{1,0:T(8,128)}, f32[32,1024]{1,0:T(8,128)S(1)}, u32[]{:S(2)}, u32[]{:S(2)}) collective-permute-start(f32[32,1024]{1,0:T(8,128)} %get-tuple-element.7), channel_id=1, source_target_pairs={{0,32},{16,48},{32,0},{48,16},{64,96},{80,112},{96,64},{112,80},{1... | collective-permute-start | bytes 393224 | tf_op jit(solution)/shard_map/ppermute | solution.py:34
  128.7 10.4 %collective-permute-start.3 = (f32[32,1024]{1,0:T(8,128)}, f32[32,1024]{1,0:T(8,128)S(1)}, u32[]{:S(2)}, u32[]{:S(2)}) collective-permute-start(f32[32,1024]{1,0:T(8,128)} %get-tuple-element.8), channel_id=1, source_target_pairs={{0,16},{16,32},{32,48},{48,0},{64,80},{80,96},{96,112},{112,64},{1... | collective-permute-start | bytes 393224 | tf_op jit(solution)/shard_map/ppermute | solution.py:34
  129.3 12.3 %collective-permute-start.4 = (f32[32,1024]{1,0:T(8,128)}, f32[32,1024]{1,0:T(8,128)S(1)}, u32[]{:S(2)}, u32[]{:S(2)}) collective-permute-start(f32[32,1024]{1,0:T(8,128)} %get-tuple-element.9), channel_id=1, source_target_pairs={{0,48},{16,0},{32,16},{48,32},{64,112},{80,64},{96,80},{112,96},{1... | collective-permute-start | bytes 393224 | tf_op jit(solution)/shard_map/ppermute | solution.py:34

commit v4 on v3

--- a/solution.py
+++ b/solution.py
@@ -34,6 +34,10 @@
     return lax.ppermute(x, "rep", [(i, i // 4 * 4 + (i + by) % 4) for i in range(16)])
 
 
+def shift(x, by):
+    return lax.ppermute(x, "rep", [(i, (i + 4 * by) % 16) for i in range(16)])
+
+
 def part(x, at, parts):
     size = x.shape[0] // parts
     return lax.dynamic_slice_in_dim(x, at * size, size, 0)
@@ -68,35 +72,36 @@
     )(at.reshape(1).astype(jnp.int32), parts, target)
 
 
-def summed_parts(x, got, side, at, by):
-    rows, cols = got.shape
+def summed_parts(x, gots, block, at, by):
+    rows, cols = gots[0].shape
     size = rows // 4
 
-    def kernel(at_ref, x_ref, got_ref, own_ref, *part_refs):
+    def kernel(at_ref, *refs):
+        ins, own_ref, part_refs = refs[:4], refs[4], refs[5:]
+
         def total(turned):
             start = pl.multiple_of((at_ref[1] + turned) % 4 * size, size)
-            return x_ref[pl.ds(start, size), :] + got_ref[pl.ds(start, size), :]
+            values = [ref[pl.ds(start, size), :].astype(f32) for ref in ins]
+            return (values[0] + values[1]) + (values[2] + values[3])
 
         own_ref[...] = total(0) * by
         for turned, part_ref in enumerate(part_refs):
             part_ref[...] = total(turned + 1)
 
     piece = jax.ShapeDtypeStruct((size, cols), f32)
+    whole = pl.BlockSpec((rows, cols), lambda i, at: (0, 0))
     return pl.pallas_call(
         kernel,
         out_shape=(piece,) * 4,
         grid_spec=pltpu.PrefetchScalarGridSpec(
             num_scalar_prefetch=1,
             grid=(1,),
-            in_specs=[
-                pl.BlockSpec((rows, cols), lambda i, at: (at[0], 0)),
-                pl.BlockSpec((rows, cols), lambda i, at: (0, 0)),
-            ],
+            in_specs=[pl.BlockSpec((rows, cols), lambda i, at: (at[0], 0)), whole, whole, whole],
             out_specs=(pl.BlockSpec((size, cols), lambda i, at: (0, 0)),) * 4,
         ),
-        cost_estimate=pl.CostEstimate(flops=rows * cols, bytes_accessed=12 * rows * cols, transcendentals=0),
+        cost_estimate=pl.CostEstimate(flops=4 * rows * cols, bytes_accessed=12 * rows * cols, transcendentals=0),
         name="summed_parts",
-    )(jnp.stack([side, at]).astype(jnp.int32), x, got)
+    )(jnp.stack([block, at]).astype(jnp.int32), x, *gots)
 
 
 def local(hidden, target, inner_weight, first_moment, second_moment, anchor, outer_momentum):
@@ -107,12 +112,11 @@
     half = hidden.shape[0] // 2
     mine, other = part(hidden, core, 2), part(hidden, 1 - core, 2)
 
-    give = part(weight, 1 - rep // 8, 2)
-    got = swap(give, "rep", 12)
-    w_x = part(weight, rep // 8, 2).astype(f32) + got.astype(f32)
-    give = part(w_x, 1 - rep // 4 % 2, 2)
-    got = swap(give, "rep", 4)
-    w_sum, *gives = summed_parts(w_x, got, rep // 4 % 2, rep % 4, 1.0 - inner_rate * decay_rate)
+    gots = []
+    for by in (2, 1, 3):
+        give = part(weight, (rep // 4 + by) % 4, 4)
+        gots.append(shift(give, by))
+    w_sum, *gives = summed_parts(weight, gots, rep // 4, rep % 4, 1.0 - inner_rate * decay_rate)
     turned = []
     for by in (2, 1, 3):
         turned.append(turn(gives[by - 1], by))

time: 177 us -> 173 us (0.977)
  other arithmetic: 6.76 us -> 3.26 us
  matrix products: 14.7 us -> 11.4 us
  starting transfers between devices: 32.1 us -> 35.3 us
    ppermute x0 -> x3, starting transfers between devices: none -> 6.76 us  [shift(): return lax.ppermute(x, 'rep', [(i, (i + 4 * by) % 16) for i in range(16)])]
    ppermute x5 -> x3, starting transfers between devices: 3.86 us -> 0.51 us  [swap(): return lax.ppermute(x, axis, [(i, i ^ mask) for i in range(16)])]
    ppermute x5 -> x3, waiting for transfers between devices: 2.4 us -> 5.59 us  [swap(): return lax.ppermute(x, axis, [(i, i ^ mask) for i in range(16)])]
    ppermute x3, waiting for transfers between devices: 8.69 us -> 6.17 us  [turn(): lax.ppermute(x, 'rep', [(i, i // 4 * 4 + (i + by) % 4) for i in range(16)])]
  transfers between devices with their start and end apart: 11 -> 12, of which waited for: 7 -> 8; matrix products, arithmetic and copies ran while one was open for 10% -> 4% of each run, Pallas kernels for 2% -> 2%
where the time goes in v4:
time: 173 us; the launch traced here: 172 us
  blocking collectives  60.5 us (35%)
  waiting for transfers between devices  49.4 us (29%)
  starting transfers between devices  35.3 us (20%)
  matrix products  11.4 us (7%)
  local copies, waits for them, and re-layouts  5.69 us (3%)
  Pallas kernels  5.38 us (3%)
  other arithmetic  3.26 us (2%)
    all_to_all x3, blocking collectives, spread(): return lax.all_to_all(x, axis, 0, 0, axis_index_groups=groups)  60.5 us
    all_to_all x3, waiting for transfers between devices, spread(): return lax.all_to_all(x, axis, 0, 0, axis_index_groups=groups)  37.6 us
    all_to_all x3, starting transfers between devices, spread(): return lax.all_to_all(x, axis, 0, 0, axis_index_groups=groups)  18 us
    ppermute x3, starting transfers between devices, turn(): lax.ppermute(x, 'rep', [(i, i // 4 * 4 + (i + by) % 4) for i in range(16)])  10.1 us
    ppermute x3, starting transfers between devices, shift(): return lax.ppermute(x, 'rep', [(i, (i + 4 * by) % 16) for i in range(16)])  6.76 us
    ppermute x3, waiting for transfers between devices, turn(): lax.ppermute(x, 'rep', [(i, i // 4 * 4 + (i + by) % 4) for i in range(16)])  6.17 us
    ppermute x3, waiting for transfers between devices, swap(): return lax.ppermute(x, axis, [(i, i ^ mask) for i in range(16)])  5.59 us
    dot_general x1, matrix products, local(): lax.dot_general(other, res_other, dims, preferred_element_type=f32)  4.72 us
  transfers between devices with their start and end apart: 12, of which 8 were waited for; matrix products, arithmetic and copies ran while one was open for 4% of the time, Pallas kernels for 2%

profile of v4, /device:TPU:8, one launch (start us, length us, event | category | flops | bytes accessed | tf_op | source)
XLA Modules:
  0.0 171.6 jit_solution(2179761620100619669)
XLA Ops:
  0.6 0.0 copy-start
  0.6 0.0 copy-start.1
  0.7 1.6 copy-done
  2.2 1.0 constant_dynamic-slice_fusion
  3.3 0.0 collective-permute-start.6
  3.3 0.0 copy-done.1
  3.3 0.5 collective-permute-start.7
  3.8 1.2 fusion.9
  5.0 1.2 collective-permute-done.6
  6.3 1.5 collective-permute-done.7
  7.8 4.1 %add_convert_fusion = bf16[1024,1024]{1,0:T(8,128)(2,1)} fusion(bf16[1024,512]{1,0:T(8,128)(2,1)} %collective-permute-done.6, bf16[512,1024]{1,0:T(8,128)(2,1)} %collective-permute-done.7, bf16[1024,1024]{1,0:T(8,128)(2,1)S(1)} %fusion.9), kind=kOutput, calls=%fused_computation | convolution fusion | flops 1076887552 | bytes 6291456 | tf_op jit(solution)/shard_map/dot_general | solution.py:127
  11.9 6.4 %all-to-all-start = ((bf16[8,128,1024]{2,1,0:T(8,128)(2,1)}), bf16[8,128,1024]{2,1,0:T(8,128)(2,1)}, u32[]{:S(2)}, u32[]{:S(2)}) async-start(bf16[8,128,1024]{2,1,0:T(8,128)(2,1)} %bitcast.57), calls=%async_computation | async-start | bytes 4194304 | tf_op jit(solution)/shard_map/all_to_all | solution.py:26
  18.3 25.6 %all-to-all-done.parts_ref = bf16[8,128,1024]{2,1,0:T(8,128)(2,1)} async-done(((bf16[8,128,1024]{2,1,0:T(8,128)(2,1)}), bf16[8,128,1024]{2,1,0:T(8,128)(2,1)}, u32[]{:S(2)}, u32[]{:S(2)}) %all-to-all-start) | async-done | bytes 2097184 | tf_op jit(solution)/shard_map/all_to_all | solution.py:26
  43.9 2.7 %residual.1 = bf16[8,128,1024]{2,1,0:T(8,128)(2,1)} custom-call(s32[1]{0:T(128)} %bitcast.8.at_ref, bf16[8,128,1024]{2,1,0:T(8,128)(2,1)} %all-to-all-done.parts_ref, bf16[2048,1024]{1,0:T(8,128)(2,1)} %goal_ref.1), custom_call_target="tpu_custom_call" | custom-call | flops 1048576 | bytes 4194304 | tf_op jit(solution)/shard_map/residual/pallas_call | solution.py:58
  46.6 30.3 %all_to_all.30 = bf16[8,128,1024]{2,1,0:T(8,128)(2,1)S(1)} all-to-all(bf16[8,128,1024]{2,1,0:T(8,128)(2,1)} %residual.1), channel_id=1, replica_groups={{0,2,4,6,8,10,12,14},{1,3,5,7,9,11,13,15},{16,18,20,22,24,26,28,30},{17..., dimensions={0} | all-to-all | bytes 4194304 | tf_op jit(solution)/shard_map/all_to_all | solution.py:26
  76.9 0.0 collective-permute-start.8
  76.9 1.3 fusion.7
  78.2 2.9 %collective-permute-done.8 = bf16[1024,1024]{1,0:T(8,128)(2,1)S(1)} collective-permute-done((bf16[1024,1024]{1,0:T(8,128)(2,1)S(1)}, bf16[1024,1024]{1,0:T(8,128)(2,1)S(1)}, u32[]{:S(2)}, u32[]{:S(2)}) %collective-permute-start.8) | collective-permute-done | bytes 2097184 | tf_op jit(solution)/shard_map/ppermute | solution.py:30
  81.1 0.0 copy-done.5
  81.1 4.7 %fusion.6 = bf16[512,1024]{1,0:T(8,128)(2,1)} fusion(f32[1,512,1024]{2,1,0:T(8,128)S(1)} %copy-done.4, f32[512,1024]{1,0:T(8,128)S(1)} %fusion.7, f32[1,512,1024]{2,1,0:T(8,128)S(1)} %copy-done.5, bf16[1024,512]{1,0:T(8,128)(2,1)} %constant_dynamic-slice_fusion, bf16[1024,1024]{1,0:T(8,128)(2,1)S(1)} %collective-permute-done.8), kind=kOutput, calls=%fused_computation.9 | convolution fusion | flops 1080557568 | bytes 10485760 | tf_op jit(solution)/shard_map/dot_general | solution.py:136
  85.8 3.9 %all-to-all-start.2 = ((bf16[4,128,1024]{2,1,0:T(8,128)(2,1)}), bf16[4,128,1024]{2,1,0:T(8,128)(2,1)S(1)}, u32[]{:S(2)}, u32[]{:S(2)}) async-start(bf16[4,128,1024]{2,1,0:T(8,128)(2,1)} %bitcast.59), calls=%async_computation.2 | async-start | bytes 2097152 | tf_op jit(solution)/shard_map/all_to_all | solution.py:26
  89.7 2.0 %dynamic-slice_bitcast_fusion = (bf16[128,1024]{1,0:T(8,128)(2,1)S(1)}, bf16[128,1024]{1,0:T(8,128)(2,1)}, bf16[128,1024]{1,0:T(8,128)(2,1)}) fusion(bf16[1,512,1024]{2,1,0:T(8,128)(2,1)} %param.9, s32[]{:T(128)S(6)} %select_n.55, s32[]{:T(128)S(6)} %select_n.51, s32[]{:T(128)S(6)} %select_n.53), kind=kLoop, calls=%fused_computation.15 | loop fusion | bytes 1572876 | tf_op jit(solution)/shard_map/dynamic_slice | solution.py:43
  91.6 3.5 %collective-permute-start = (bf16[128,1024]{1,0:T(8,128)(2,1)}, bf16[128,1024]{1,0:T(8,128)(2,1)}, u32[]{:S(2)}, u32[]{:S(2)}) collective-permute-start(bf16[128,1024]{1,0:T(8,128)(2,1)} %get-tuple-element.11), channel_id=1, source_target_pairs={{0,128},{16,144},{32,160},{48,176},{64,192},{80,208},{96,224},{112... | collective-permute-start | bytes 786440 | tf_op jit(solution)/shard_map/ppermute | solution.py:38
  95.2 0.6 collective-permute-start.1
  95.7 2.7 %collective-permute-start.2 = (bf16[128,1024]{1,0:T(8,128)(2,1)S(1)}, bf16[128,1024]{1,0:T(8,128)(2,1)}, u32[]{:S(2)}, u32[]{:S(2)}) collective-permute-start(bf16[128,1024]{1,0:T(8,128)(2,1)S(1)} %get-tuple-element.10), channel_id=1, source_target_pairs={{0,192},{16,208},{32,224},{48,240},{64,0},{80,16},{96,32},{112,48}... | collective-permute-start | bytes 786440 | tf_op jit(solution)/shard_map/ppermute | solution.py:38
  98.4 12.0 %all-to-all-done.2 = bf16[4,128,1024]{2,1,0:T(8,128)(2,1)S(1)} async-done(((bf16[4,128,1024]{2,1,0:T(8,128)(2,1)}), bf16[4,128,1024]{2,1,0:T(8,128)(2,1)S(1)}, u32[]{:S(2)}, u32[]{:S(2)}) %all-to-all-start.2) | async-done | bytes 1048608 | tf_op jit(solution)/shard_map/all_to_all | solution.py:26
  110.4 0.9 reduce_sum.21
  111.4 7.7 %all-to-all-start.3 = ((bf16[4,32,1024]{2,1,0:T(8,128)(2,1)}), bf16[4,32,1024]{2,1,0:T(8,128)(2,1)S(1)}, u32[]{:S(2)}, u32[]{:S(2)}) async-start(bf16[4,32,1024]{2,1,0:T(8,128)(2,1)} %bitcast.13), calls=%async_computation.3 | async-start | bytes 524288 | tf_op jit(solution)/shard_map/all_to_all | solution.py:26
  119.0 0.6 pad_add_fusion.at_ref
  119.7 0.0 collective-permute-done.refs_1_
  119.7 0.0 collective-permute-done.1.refs_2_
  119.7 0.0 collective-permute-done.2.refs_3_
  119.7 2.7 %summed_parts.1 = (f32[32,1024]{1,0:T(8,128)}, f32[32,1024]{1,0:T(8,128)}, f32[32,1024]{1,0:T(8,128)}, f32[32,1024]{1,0:T(8,128)}) custom-call(s32[2]{0:T(128)} %pad_add_fusion.at_ref, bf16[512,1024]{1,0:T(8,128)(2,1)} %bitcast.55, bf16[128,1024]{1,0:T(8,128)(2,1)} %collective-permute-done.refs_1_, bf16[128,1024]{1,0:T(8,128)(2,1)} %collective-permute-done.1.refs_2_, ...), custom_call_target="tpu_custom_call" | custom-call | flops 524288 | bytes 1572864 | tf_op jit(solution)/shard_map/summed_parts/pallas_call | solution.py:93
  122.4 5.9 %collective-permute-start.3 = (f32[32,1024]{1,0:T(8,128)}, f32[32,1024]{1,0:T(8,128)S(1)}, u32[]{:S(2)}, u32[]{:S(2)}) collective-permute-start(f32[32,1024]{1,0:T(8,128)} %get-tuple-element.7), channel_id=1, source_target_pairs={{0,32},{16,48},{32,0},{48,16},{64,96},{80,112},{96,64},{112,80},{1... | collective-permute-start | bytes 393224 | tf_op jit(solution)/shard_map/ppermute | solution.py:34
  128.3 0.6 collective-permute-start.4
  128.9 3.6 %collective-permute-start.5 = (f32[32,1024]{1,0:T(8,128)}, f32[32,1024]{1,0:T(8,128)S(1)}, u32[]{:S(2)}, u32[]{:S(2)}) collective-permute-start(f32[32,1024]{1,0:T(8,128)} %get-tuple-element.9), channel_id=1, source_target_pairs={{0,48},{16,0},{32,16},{48,32},{64,112},{80,64},{96,80},{112,96},{1... | collective-permute-start | bytes 393224 | tf_op jit(solution)/shard_map/ppermute | solution.py:34
  132.4 4.2 %collective-permute-done.3 = f32[32,1024]{1,0:T(8,128)S(1)} collective-permute-done((f32[32,1024]{1,0:T(8,128)}, f32[32,1024]{1,0:T(8,128)S(1)}, u32[]{:S(2)}, u32[]{:S(2)}) %collective-permute-start.3) | collective-permute-done | bytes 131104 | tf_op jit(solution)/shard_map/ppermute | solution.py:34
  136.6 0.8 collective-permute-done.4
  137.4 1.2 collective-permute-done.5
  138.6 0.9 multiply_add_fusion
  139.5 0.0 all-to-all-done.3
  139.6 0.0 copy-done.2
  139.6 0.0 copy-done.3
  139.6 0.7 fusion.12
  140.4 14.7 %all_to_all.31 = bf16[4,32,1024]{2,1,0:T(8,128)(2,1)S(1)} all-to-all(bf16[4,32,1024]{2,1,0:T(8,128)(2,1)S(1)} %broadcast_in_dim.16), channel_id=1, replica_groups={{0,16,32,48},{64,80,96,112},{128,144,160,176},{192,208,224,240},{1,17,3..., dimensions={0} | all-to-all | bytes 524288 | tf_op jit(solution)/shard_map/all_to_all | solution.py:26
  155.0 0.1 broadcast_in_dim.18
  155.1 15.5 %all_to_all.32 = bf16[4,128,1024]{2,1,0:T(8,128)(2,1)S(1)} all-to-all(bf16[4,128,1024]{2,1,0:T(8,128)(2,1)S(1)} %broadcast_in_dim.18), channel_id=1, replica_groups={{0,64,128,192},{16,80,144,208},{32,96,160,224},{48,112,176,240},{1,65,1..., dimensions={0} | all-to-all | bytes 2097152 | tf_op jit(solution)/shard_map/all_to_all | solution.py:26
  170.6 1.0 copy.10
  (7 shorter events, 0.1 us)
Async XLA Ops:
  0.6 1.6 copy-start
  0.6 2.6 %copy-start.1 = (bf16[1,512,1024]{2,1,0:T(8,128)(2,1)S(1)}, bf16[1,512,1024]{2,1,0:T(8,128)(2,1)}, u32[]{:S(2)}) copy-start(bf16[1,512,1024]{2,1,0:T(8,128)(2,1)} %param.9) | copy-start | bytes 3145732
  3.3 3.0 %collective-permute-start.6 = (bf16[1024,512]{1,0:T(8,128)(2,1)}, bf16[1024,512]{1,0:T(8,128)(2,1)}, u32[]{:S(2)}, u32[]{:S(2)}) collective-permute-start(bf16[1024,512]{1,0:T(8,128)(2,1)} %constant_dynamic-slice_fusion), channel_id=1, source_target_pairs={{0,1},{1,0},{2,3},{3,2},{4,5},{5,4},{6,7},{7,6},{8,9},{9,8},{10,11... | collective-permute-start | bytes 3145736 | tf_op jit(solution)/shard_map/ppermute | solution.py:30
  3.3 4.5 %collective-permute-start.7 = (bf16[512,1024]{1,0:T(8,128)(2,1)S(1)}, bf16[512,1024]{1,0:T(8,128)(2,1)}, u32[]{:S(2)}, u32[]{:S(2)}) collective-permute-start(bf16[512,1024]{1,0:T(8,128)(2,1)S(1)} %bitcast.56), channel_id=1, source_target_pairs={{0,1},{1,0},{2,3},{3,2},{4,5},{5,4},{6,7},{7,6},{8,9},{9,8},{10,11... | collective-permute-start | bytes 3145736 | tf_op jit(solution)/shard_map/ppermute | solution.py:30
  11.9 32.0 %all-to-all-start = ((bf16[8,128,1024]{2,1,0:T(8,128)(2,1)}), bf16[8,128,1024]{2,1,0:T(8,128)(2,1)}, u32[]{:S(2)}, u32[]{:S(2)}) async-start(bf16[8,128,1024]{2,1,0:T(8,128)(2,1)} %bitcast.57), calls=%async_computation | async-start | bytes 4194304 | tf_op jit(solution)/shard_map/all_to_all | solution.py:26
  76.9 4.2 %copy-start.4 = (f32[1,512,1024]{2,1,0:T(8,128)S(1)}, f32[1,512,1024]{2,1,0:T(8,128)}, u32[]{:S(2)}) copy-start(f32[1,512,1024]{2,1,0:T(8,128)} %param.11) | copy-start | bytes 6291460
  76.9 4.2 %copy-start.5 = (f32[1,512,1024]{2,1,0:T(8,128)S(1)}, f32[1,512,1024]{2,1,0:T(8,128)}, u32[]{:S(2)}) copy-start(f32[1,512,1024]{2,1,0:T(8,128)} %param.10) | copy-start | bytes 6291460
  76.9 4.2 %collective-permute-start.8 = (bf16[1024,1024]{1,0:T(8,128)(2,1)S(1)}, bf16[1024,1024]{1,0:T(8,128)(2,1)S(1)}, u32[]{:S(2)}, u32[]{:S(2)}) collective-permute-start(bf16[1024,1024]{1,0:T(8,128)(2,1)S(1)} %bitcast.52), channel_id=1, source_target_pairs={{0,1},{1,0},{2,3},{3,2},{4,5},{5,4},{6,7},{7,6},{8,9},{9,8},{10,11... | collective-permute-start | bytes 6291464 | tf_op jit(solution)/shard_map/ppermute | solution.py:30
  85.8 24.6 %all-to-all-start.2 = ((bf16[4,128,1024]{2,1,0:T(8,128)(2,1)}), bf16[4,128,1024]{2,1,0:T(8,128)(2,1)S(1)}, u32[]{:S(2)}, u32[]{:S(2)}) async-start(bf16[4,128,1024]{2,1,0:T(8,128)(2,1)} %bitcast.59), calls=%async_computation.2 | async-start | bytes 2097152 | tf_op jit(solution)/shard_map/all_to_all | solution.py:26
  91.6 28.1 %collective-permute-start = (bf16[128,1024]{1,0:T(8,128)(2,1)}, bf16[128,1024]{1,0:T(8,128)(2,1)}, u32[]{:S(2)}, u32[]{:S(2)}) collective-permute-start(bf16[128,1024]{1,0:T(8,128)(2,1)} %get-tuple-element.11), channel_id=1, source_target_pairs={{0,128},{16,144},{32,160},{48,176},{64,192},{80,208},{96,224},{112... | collective-permute-start | bytes 786440 | tf_op jit(solution)/shard_map/ppermute | solution.py:38
  95.2 24.5 %collective-permute-start.1 = (bf16[128,1024]{1,0:T(8,128)(2,1)}, bf16[128,1024]{1,0:T(8,128)(2,1)}, u32[]{:S(2)}, u32[]{:S(2)}) collective-permute-start(bf16[128,1024]{1,0:T(8,128)(2,1)} %get-tuple-element.12), channel_id=1, source_target_pairs={{0,64},{16,80},{32,96},{48,112},{64,128},{80,144},{96,160},{112,17... | collective-permute-start | bytes 786440 | tf_op jit(solution)/shard_map/ppermute | solution.py:38
  95.7 24.0 %collective-permute-start.2 = (bf16[128,1024]{1,0:T(8,128)(2,1)S(1)}, bf16[128,1024]{1,0:T(8,128)(2,1)}, u32[]{:S(2)}, u32[]{:S(2)}) collective-permute-start(bf16[128,1024]{1,0:T(8,128)(2,1)S(1)} %get-tuple-element.10), channel_id=1, source_target_pairs={{0,192},{16,208},{32,224},{48,240},{64,0},{80,16},{96,32},{112,48}... | collective-permute-start | bytes 786440 | tf_op jit(solution)/shard_map/ppermute | solution.py:38
  98.4 41.2 %copy-start.2 = (f32[1,32,1024]{2,1,0:T(8,128)S(1)}, f32[1,32,1024]{2,1,0:T(8,128)}, u32[]{:S(2)}) copy-start(f32[1,32,1024]{2,1,0:T(8,128)} %param.13) | copy-start | bytes 393220
  111.4 28.3 %copy-start.3 = (f32[1,32,1024]{2,1,0:T(8,128)S(1)}, f32[1,32,1024]{2,1,0:T(8,128)}, u32[]{:S(2)}) copy-start(f32[1,32,1024]{2,1,0:T(8,128)} %param.12) | copy-start | bytes 393220
  111.4 28.2 %all-to-all-start.3 = ((bf16[4,32,1024]{2,1,0:T(8,128)(2,1)}), bf16[4,32,1024]{2,1,0:T(8,128)(2,1)S(1)}, u32[]{:S(2)}, u32[]{:S(2)}) async-start(bf16[4,32,1024]{2,1,0:T(8,128)(2,1)} %bitcast.13), calls=%async_computation.3 | async-start | bytes 524288 | tf_op jit(solution)/shard_map/all_to_all | solution.py:26
  122.4 14.2 %collective-permute-start.3 = (f32[32,1024]{1,0:T(8,128)}, f32[32,1024]{1,0:T(8,128)S(1)}, u32[]{:S(2)}, u32[]{:S(2)}) collective-permute-start(f32[32,1024]{1,0:T(8,128)} %get-tuple-element.7), channel_id=1, source_target_pairs={{0,32},{16,48},{32,0},{48,16},{64,96},{80,112},{96,64},{112,80},{1... | collective-permute-start | bytes 393224 | tf_op jit(solution)/shard_map/ppermute | solution.py:34
  128.3 9.1 %collective-permute-start.4 = (f32[32,1024]{1,0:T(8,128)}, f32[32,1024]{1,0:T(8,128)S(1)}, u32[]{:S(2)}, u32[]{:S(2)}) collective-permute-start(f32[32,1024]{1,0:T(8,128)} %get-tuple-element.8), channel_id=1, source_target_pairs={{0,16},{16,32},{32,48},{48,0},{64,80},{80,96},{96,112},{112,64},{1... | collective-permute-start | bytes 393224 | tf_op jit(solution)/shard_map/ppermute | solution.py:34
  128.9 9.7 %collective-permute-start.5 = (f32[32,1024]{1,0:T(8,128)}, f32[32,1024]{1,0:T(8,128)S(1)}, u32[]{:S(2)}, u32[]{:S(2)}) collective-permute-start(f32[32,1024]{1,0:T(8,128)} %get-tuple-element.9), channel_id=1, source_target_pairs={{0,48},{16,0},{32,16},{48,32},{64,112},{80,64},{96,80},{112,96},{1... | collective-permute-start | bytes 393224 | tf_op jit(solution)/shard_map/ppermute | solution.py:34
